TPU v7x, 256 devices: a whole 4x4x8 slice. The times are simulated.
256 devices in a mesh: tm: 8 (over x, core), stn: 32 (over z, y).
Axes of the slice: x: 4, y: 4, z: 8, core: 2. Of those that a mesh axis runs over, the one named last changes fastest.
Arguments:
- voltages: bfloat16 [512, 2, 165888], P('stn', None, 'tm'), may hold values from -6 to 6
- prototype: float32 [12, 768], replicated, may hold values from -1.75 to 1.75
- kept_channels: int32 [64], replicated, may hold values from 0 to 383, as said below
- beam_jones: float32 [512, 2, 2, 2, 64], P('stn'), may hold values from -3 to 3
- station_map: int32 [512], replicated, may hold values from 0 to 511, each once
- tile_pairs: int32 [36, 2], replicated, may hold values from 0 to 7, as said below
Outputs:
- visibilities: float32 [256, 36, 2, 128, 128], P(('tm', 'stn'))
Inputs may be any that keep to these rules, and one draw needn't show every extreme that they name: `kept_channels`: distinct coarse channel numbers in no particular order; channel 0 and the highest channel are always among them. Each row of voltages and beam_jones belongs to station station_map[row]; every station once. `tile_pairs`: every unordered pair of signal blocks, a block with itself included, stands in exactly one row, in either order.
All inputs are finite; a program needn't handle non-finite values.
Results may differ from a plain program's by a relative error of at most 0.0037.
Values may be sent and summed in bfloat16 or wider, within the bound.
No kernel may reach another device: no remote copies, remote signals or barrier semaphores. Data moves between devices by JAX's collectives and lax.ppermute only.
A program may use at most 64 MiB of HBM per device.

v0:
```python
import functools
import math

import jax
import jax.numpy as jnp
import numpy as np
from jax import lax
from jax.experimental import pallas as pl
from jax.experimental.pallas import tpu as pltpu
from jax.sharding import PartitionSpec as P

GROUP = 54
BLOCK = 128
TAPS = 12
FRAME = 768
COLS = FRAME // 128
LOCAL = 27
EDGE = 12
SIGS = 32
KEPT = 64
ROWS = 56

F32 = jnp.float32
BF16 = jnp.bfloat16
NT = (((1,), (1,)), ((), ()))
NN = (((1,), (0,)), ((), ()))


def vmem():
    return pl.BlockSpec(memory_space=pltpu.VMEM)


def anywhere():
    return pl.BlockSpec(memory_space=pl.ANY)


def smem():
    return pl.BlockSpec(memory_space=pltpu.SMEM)


def split(value):
    high = value.astype(BF16)
    return high, (value - high.astype(F32)).astype(BF16)


def fetch(x_ref, buf, sems, col, first, count):
    stations = buf.shape[2]
    return [
        pltpu.make_async_copy(
            x_ref.at[s, pl.ds(first, count), col], buf.at[col, :, s], sems.at[col, s]
        )
        for s in range(stations)
    ]


def coarse_table(kept_ref, w_ref):
    kept = jnp.broadcast_to(kept_ref[...], (KEPT, 128))
    lane = lax.broadcasted_iota(jnp.int32, (KEPT, 128), 1)

    def turn(phase):
        whole = jnp.floor(phase.astype(F32) * (1.0 / FRAME)).astype(jnp.int32)
        angle = (phase - whole * FRAME).astype(F32) * (2.0 * math.pi / FRAME)
        return jnp.cos(angle), -jnp.sin(angle)

    re, im = turn(kept * lane)
    factor = 1.0 / math.sqrt(FRAME)
    re, im = re * factor, im * factor
    step_re, step_im = turn(kept * 128)
    for col in range(COLS):
        span = slice(col * 128, col * 128 + 128)
        for part, value in enumerate((re, im)):
            high, low = split(value)
            w_ref[part * KEPT : part * KEPT + KEPT, span] = high
            w_ref[128 + part * KEPT : 128 + part * KEPT + KEPT, span] = low
        re, im = re * step_re - im * step_im, re * step_im + im * step_re


def filter_column(load, proto_ref, high_ref, low_ref, col, half, sources, outputs):
    lanes = pl.ds(pl.multiple_of(col * 128, 128), 128)
    taps = [jnp.broadcast_to(proto_ref[k : k + 1, lanes], (16, 128)) for k in range(TAPS)]
    sums, left = {}, {}
    for n in sources:
        for k in range(TAPS):
            if (k, n) in outputs:
                left[outputs[k, n]] = left.get(outputs[k, n], 0) + 1
    for n in sources:
        x = load(n, col, half).astype(F32)
        for k in range(TAPS):
            if (k, n) not in outputs:
                continue
            out = outputs[k, n]
            sums[out] = sums[out] + taps[k] * x if out in sums else taps[k] * x
            left[out] -= 1
            if left[out] == 0:
                high, low = split(sums.pop(out))
                rows = pl.ds(pl.multiple_of(out * SIGS + half * 16, 16), 16)
                high_ref[rows, lanes] = high
                low_ref[rows, lanes] = low


def run_filter(x_ref, buf, sems, proto_ref, high_ref, low_ref, first, count, outputs):
    copies = [fetch(x_ref, buf, sems, col, first, count) for col in range(COLS)]
    for group in copies:
        for copy in group:
            copy.start()
    view = buf.reshape(COLS, count, SIGS, 128)

    def load(n, col, half):
        return view[col, n, pl.ds(pl.multiple_of(half * 16, 16), 16), :]

    for col in range(COLS):
        for copy in copies[col]:
            copy.wait()

        @pl.loop(0, 2)
        def _(half):
            filter_column(load, proto_ref, high_ref, low_ref, col, half, range(count), outputs)


def spectrum(w_ref, high_ref, low_ref, first, count):
    rows = slice(first, first + count)
    both = lax.dot_general(w_ref[...], high_ref[rows, :], NT, preferred_element_type=F32)
    rest = lax.dot_general(w_ref[:128, :], low_ref[rows, :], NT, preferred_element_type=F32)
    return both[:128] + both[128:] + rest


def beam_and_deal(load, jones_ref, dealt_ref, tiles, tile_at, stride):
    lane = lax.broadcasted_iota(jnp.int32, (8, 128), 1)
    even = lane % 2 == 0
    low_half = lane < 64
    even_chunk = (lane // 32) % 2 == 0

    def swap(value):
        return jnp.where(even, pltpu.roll(value, 127, 1), pltpu.roll(value, 1, 1))

    def beam(tile, row):
        re, im = load(row, tile), load(KEPT + row, tile)
        swap_re, swap_im = swap(re), swap(im)
        own_re, own_im, cross_re, cross_im = (
            jones_ref[n * KEPT + row : n * KEPT + row + 8, :] for n in range(4)
        )
        return (
            own_re * re - own_im * im + cross_re * swap_re - cross_im * swap_im,
            own_re * im + own_im * re + cross_re * swap_im + cross_im * swap_re,
        )

    for tile in range(tiles):
        for h in range(2):
            beams = [beam(tile, (j * 2 + h) * 8) for j in range(4)]
            for part in range(2):
                v = [beams[j][part] for j in range(4)]
                u = [None] * 4
                for j in range(2):
                    u[j] = jnp.where(low_half, v[j], pltpu.roll(v[j + 2], 64, 1))
                    u[j + 2] = jnp.where(low_half, pltpu.roll(v[j], 64, 1), v[j + 2])
                for i in (0, 2):
                    first = jnp.where(even_chunk, u[i], pltpu.roll(u[i + 1], 32, 1))
                    second = jnp.where(even_chunk, pltpu.roll(u[i], 96, 1), u[i + 1])
                    for n, value in enumerate((first, second)):
                        frame = (tile_at + tile) * 4 + i + n
                        row = h * (stride // 2) + (frame - tile_at * 4) * 2 + part
                        dealt_ref[pl.ds(row, 8, stride=stride), :] = value


MAIN_OUT = {
    (k, n): n + TAPS - 1 - k
    for n in range(LOCAL)
    for k in range(TAPS)
    if n + TAPS - 1 - k < LOCAL
}


def halo_outputs():
    return {(k, f + k): f for f in range(11) for k in range(TAPS) if f + k <= 10}


def halo_kernel(x_ref, proto_ref, kept_ref, w_ref, out_ref, buf, sems, high_ref, low_ref):
    coarse_table(kept_ref, w_ref)
    zero = jnp.zeros((SIGS, FRAME), BF16)
    high_ref[11 * SIGS :, :] = zero
    low_ref[11 * SIGS :, :] = zero
    run_filter(
        x_ref, buf, sems, proto_ref, high_ref, low_ref, LOCAL - 11, 11, halo_outputs()
    )
    out_ref[...] = spectrum(w_ref, high_ref, low_ref, 0, EDGE * SIGS)


def main_kernel(
    x_ref, proto_ref, w_ref, beam_ref, edge_ref, jones_ref, out_ref,
    buf, sems, high_ref, low_ref, coarse_ref, dealt_ref, turned_ref,
):
    side = lax.broadcasted_iota(jnp.int32, (KEPT, 128), 1) % 2 == 0
    for part in range(2):
        for q in range(2):
            rows = beam_ref[pl.ds(q * 2 + part, SIGS, stride=4), :]
            wide = jnp.concatenate([rows.T] * 4, axis=1)
            turned_ref[q * KEPT : q * KEPT + KEPT, :] = wide
        for j in range(4):
            for h in range(2):
                first = turned_ref[pl.ds(4 * h + j, 8, stride=8), :]
                second = turned_ref[pl.ds(KEPT + 4 * h + j, 8, stride=8), :]
                row = (j * 2 + h) * 8
                own = jnp.where(side[:8], first, second)
                cross = jnp.where(side[:8], second, first)
                jones_ref[part * KEPT + row : part * KEPT + row + 8, :] = own
                jones_ref[(2 + part) * KEPT + row : (2 + part) * KEPT + row + 8, :] = cross
    zero = jnp.zeros((SIGS, FRAME), BF16)
    high_ref[LOCAL * SIGS :, :] = zero
    low_ref[LOCAL * SIGS :, :] = zero
    run_filter(x_ref, buf, sems, proto_ref, high_ref, low_ref, 0, LOCAL, MAIN_OUT)
    edge_ref[...] = spectrum(w_ref, high_ref, low_ref, 0, EDGE * SIGS)
    coarse_ref[...] = spectrum(w_ref, high_ref, low_ref, EDGE * SIGS, (LOCAL + 1 - EDGE) * SIGS)
    beam_and_deal(
        lambda row, tile: coarse_ref[row : row + 8, tile * 128 : tile * 128 + 128],
        jones_ref, dealt_ref, 4, 3, 64,
    )
    for d in range(8):
        for h in range(2):
            out_ref[d, h] = dealt_ref[d * 64 + h * 32 : d * 64 + h * 32 + 32, :].astype(BF16)


def edge_kernel(halo_ref, edge_ref, jones_ref, rest_ref, out_ref, dealt_ref):
    def load(row, tile):
        span = slice(tile * 128, tile * 128 + 128)
        return halo_ref[row : row + 8, span] + edge_ref[row : row + 8, span]

    beam_and_deal(load, jones_ref, dealt_ref, 3, 0, 48)
    for d in range(8):
        for h in range(2):
            out_ref[d, h, 0:24, :] = dealt_ref[d * 48 + h * 24 : d * 48 + h * 24 + 24, :].astype(BF16)
            out_ref[d, h, 24:56, :] = rest_ref[d, h]


def fine_table():
    blocks, frames = 8, LOCAL
    length = blocks * frames
    k = np.arange(length)
    angle = 2.0 * np.pi * ((k[:, None] * k[None, :]) % length) / length
    cosine = np.cos(angle) / np.sqrt(length)
    sine = np.sin(angle) / np.sqrt(length)
    groups = length // GROUP
    table = np.zeros((blocks, ROWS, groups, 128))
    view = table[:, : 2 * frames].reshape(blocks, frames, 2, groups, 128)
    cosine = cosine.reshape(blocks, frames, groups, GROUP)
    sine = sine.reshape(blocks, frames, groups, GROUP)
    view[:, :, 0, :, :GROUP] = cosine
    view[:, :, 1, :, :GROUP] = sine
    view[:, :, 0, :, GROUP : 2 * GROUP] = -sine
    view[:, :, 1, :, GROUP : 2 * GROUP] = cosine
    table[:, : 2 * frames] = view.reshape(blocks, 2 * frames, groups, 128)
    table = table.reshape(blocks * ROWS, groups * 128).astype(np.float32)
    high = table.astype(jnp.bfloat16)
    low = (table - high.astype(np.float32)).astype(jnp.bfloat16)
    return np.stack([high, low])


def fine_kernel(x_ref, table_ref, out_ref):
    for h in range(2):
        rows = x_ref[:, h].astype(F32).reshape(8 * ROWS, 128)
        turned = rows.T.astype(BF16)
        fine = lax.dot_general(turned, table_ref[0], NN, preferred_element_type=F32)
        fine = fine + lax.dot_general(turned, table_ref[1], NN, preferred_element_type=F32)
        for j in range(4):
            for g in range(4):
                piece = fine[j * 32 : j * 32 + 32, g * 128 : g * 128 + 128]
                out_ref[(h * 4 + j) * 4 + g] = piece.astype(BF16)


PER_STEP = 4


def pairs_kernel(map_ref, pairs_ref, x_ref, out_ref, ordered_ref, turned_ref):
    step = pl.program_id(0)
    rows = ordered_ref.reshape(1024, 128)

    @pl.when(step == 0)
    def _():
        @pl.loop(0, 512, unroll=8)
        def _(row):
            ordered_ref[map_ref[row]] = x_ref[row]

        lane = lax.broadcasted_iota(jnp.int32, (128, 128), 1)
        for block in range(8):
            value = rows[block * 128 : block * 128 + 128, :].astype(F32)
            turned = jnp.where(
                lane < GROUP, -pltpu.roll(value, 128 - GROUP, 1), pltpu.roll(value, GROUP, 1)
            )
            turned_ref[block * 128 : block * 128 + 128, :] = turned.astype(BF16)

    for n in range(PER_STEP):
        left = pl.ds(pl.multiple_of(pairs_ref[2 * (step * PER_STEP + n)] * 128, 128), 128)
        right = pl.ds(pl.multiple_of(pairs_ref[2 * (step * PER_STEP + n) + 1] * 128, 128), 128)
        own = rows[left, :]
        other = jnp.concatenate([rows[right, :], turned_ref[right, :]], axis=0)
        product = lax.dot_general(own, other, NT, preferred_element_type=F32) * (1.0 / GROUP)
        out_ref[0, n, 0] = product[:, :128]
        out_ref[0, n, 1] = product[:, 128:]


def halo_call(x, proto, kept):
    return pl.pallas_call(
        halo_kernel,
        out_shape=(
            jax.ShapeDtypeStruct((256, FRAME), BF16),
            jax.ShapeDtypeStruct((128, EDGE * SIGS), F32),
        ),
        in_specs=[anywhere(), vmem(), vmem()],
        out_specs=(vmem(), vmem()),
        scratch_shapes=[
            pltpu.VMEM((COLS, 11, 16, 2, 128), BF16),
            pltpu.SemaphoreType.DMA((COLS, 16)),
            pltpu.VMEM((EDGE * SIGS, FRAME), BF16),
            pltpu.VMEM((EDGE * SIGS, FRAME), BF16),
        ],
        name="halo",
    )(x, proto, kept)


def main_call(x, proto, table, jones):
    rows = (LOCAL + 1) * SIGS
    return pl.pallas_call(
        main_kernel,
        out_shape=(
            jax.ShapeDtypeStruct((128, EDGE * SIGS), F32),
            jax.ShapeDtypeStruct((4 * KEPT, 128), F32),
            jax.ShapeDtypeStruct((8, 2, 32, 128), BF16),
        ),
        in_specs=[anywhere(), vmem(), vmem(), vmem()],
        out_specs=(vmem(), vmem(), vmem()),
        scratch_shapes=[
            pltpu.VMEM((COLS, LOCAL, 16, 2, 128), BF16),
            pltpu.SemaphoreType.DMA((COLS, 16)),
            pltpu.VMEM((rows, FRAME), BF16),
            pltpu.VMEM((rows, FRAME), BF16),
            pltpu.VMEM((128, rows - EDGE * SIGS), F32),
            pltpu.VMEM((8 * 64, 128), F32),
            pltpu.VMEM((2 * KEPT, 128), F32),
        ],
        cost_estimate=pl.CostEstimate(flops=10**9, bytes_accessed=4 * 10**6, transcendentals=0),
        name="main",
    )(x, proto, table, jones)


def edge_call(halo, edge, jones, rest):
    return pl.pallas_call(
        edge_kernel,
        out_shape=jax.ShapeDtypeStruct((8, 2, ROWS, 128), BF16),
        in_specs=[vmem()] * 4,
        out_specs=vmem(),
        scratch_shapes=[pltpu.VMEM((8 * 48, 128), F32)],
        name="edge",
    )(halo, edge, jones, rest)


def fine_call(turned, table):
    return pl.pallas_call(
        fine_kernel,
        out_shape=jax.ShapeDtypeStruct((32, SIGS, 128), BF16),
        in_specs=[vmem()] * 2,
        out_specs=vmem(),
        name="fine",
    )(turned, table)


def pairs_call(station_map, tile_pairs, rows):
    tiles = tile_pairs.shape[0] // 2
    return pl.pallas_call(
        pairs_kernel,
        grid=(tiles // PER_STEP,),
        out_shape=jax.ShapeDtypeStruct((1, tiles, 2, BLOCK, BLOCK), F32),
        in_specs=[smem(), smem(), vmem()],
        out_specs=pl.BlockSpec((1, PER_STEP, 2, BLOCK, BLOCK), lambda i: (0, i, 0, 0, 0)),
        scratch_shapes=[pltpu.VMEM((512, 2, 128), BF16), pltpu.VMEM((1024, 128), BF16)],
        name="pairs",
    )(station_map, tile_pairs, rows)


def shards(voltages, prototype, kept_channels, beam_jones, station_map, tile_pairs):
    stations = voltages.shape[0]
    x = voltages.reshape(stations, 2, LOCAL * COLS, 128).transpose(0, 2, 1, 3)
    x = x.reshape(stations, LOCAL, COLS, 2, 128)
    kept = kept_channels.reshape(8, 2, 4).transpose(2, 1, 0).reshape(KEPT, 1)
    table, halo = halo_call(x, prototype, kept)
    blocks = lax.axis_size("tm")
    halo = lax.ppermute(halo, "tm", [(n, n + 1) for n in range(blocks - 1)])
    edge, jones, rest = main_call(x, prototype, table, beam_jones.reshape(128, KEPT))
    beamed = edge_call(halo, edge, jones, rest)
    turned = lax.all_to_all(beamed, "tm", 0, 0, tiled=True)
    fine = fine_call(turned, jnp.asarray(fine_table()))
    fine = fine.reshape(32, 16, 2, 128)
    rows = lax.all_to_all(fine, "stn", 0, 0, tiled=True)
    return pairs_call(station_map, tile_pairs.reshape(-1), rows.reshape(512, 2, 128))


def solution(mesh):
    placed = (P("stn", None, "tm"), P(), P(), P("stn", None, None, None, None), P(), P())
    return jax.shard_map(
        shards,
        mesh=mesh,
        in_specs=placed,
        out_specs=P(("tm", "stn"), None, None, None, None),
        check_vma=False,
    )
```

profile of v0, /device:TPU:32, one launch (start us, length us, event | category | flops | bytes accessed | tf_op | source)
XLA Modules:
  0.0 70.8 jit_solution(8361609328892897844)
XLA Ops:
  0.0 0.7 %reshape.27 = s32[8,2,4]{2,1,0:T(2,128)S(1)} reshape(s32[64]{0:T(128)} %param.9) | data formatting | bytes 512 | tf_op jit(solution)/shard_map/reshape | solution.py:382
  0.7 0.1 copy.15
  0.8 0.7 reshape.33.kept_ref
  1.5 3.6 %reshape.32 = bf16[16,2,162,128]{3,2,1,0:T(8,128)(2,1)S(1)} reshape(bf16[16,2,20736]{2,1,0:T(2,128)(2,1)} %param.7) | data formatting | bytes 2654208 | tf_op jit(solution)/shard_map/reshape | solution.py:380
  5.2 2.1 %copy.14 = bf16[16,162,2,128]{3,2,1,0:T(2,128)(2,1)} copy(bf16[16,162,2,128]{3,1,2,0:T(8,128)(2,1)S(1)} %bitcast.7) | data formatting | bytes 2654208 | tf_op jit(solution)/shard_map/transpose | solution.py:380
  7.3 4.7 %halo.1 = (bf16[256,768]{1,0:T(8,128)(2,1)}, f32[128,384]{1,0:T(8,128)}) custom-call(bf16[16,27,6,2,128]{4,3,2,1,0:T(2,128)(2,1)} %bitcast.8, f32[12,768]{1,0:T(8,128)} %proto_ref.3, s32[64,1]{1,0:T(8,128)} %reshape.33.kept_ref), custom_call_target="tpu_custom_call" | custom-call | tf_op jit(solution)/shard_map/halo/pallas_call | solution.py:301
  12.0 1.8 %collective-permute-start = (f32[128,384]{1,0:T(8,128)}, f32[128,384]{1,0:T(8,128)S(1)}, u32[]{:S(2)}, u32[]{:S(2)}) collective-permute-start(f32[128,384]{1,0:T(8,128)} %get-tuple-element.10), channel_id=1, source_target_pairs={{0,32},{32,64},{64,96},{96,128},{128,160},{160,192},{192,224},{1,3... | collective-permute-start | bytes 589832 | tf_op jit(solution)/shard_map/ppermute | solution.py:385
  13.8 7.7 %main.1 = (f32[128,384]{1,0:T(8,128)}, f32[256,128]{1,0:T(8,128)}, bf16[8,2,32,128]{3,2,1,0:T(8,128)(2,1)}) custom-call(bf16[16,27,6,2,128]{4,3,2,1,0:T(2,128)(2,1)} %bitcast.9, f32[12,768]{1,0:T(8,128)} %proto_ref.3, bf16[256,768]{1,0:T(8,128)(2,1)} %get-tuple-element.11.w_ref, f32[128,64]{1,0:T(8,128)} %bitcast.13), custom_call_target="tpu_custom_call" | custom-call | flops 1000000000 | bytes 4000000 | tf_op jit(solution)/shard_map/main/pallas_call | solution.py:321
  21.5 0.0 collective-permute-done.halo_ref
  21.5 0.0 copy-start.1
  21.5 0.7 copy-done.1
  22.2 2.2 %edge.1 = bf16[8,2,56,128]{3,2,1,0:T(8,128)(2,1)} custom-call(f32[128,384]{1,0:T(8,128)} %copy-done.1, f32[128,384]{1,0:T(8,128)} %get-tuple-element.12.edge_ref, f32[256,128]{1,0:T(8,128)} %get-tuple-element.13.jones_ref, bf16[8,2,32,128]{3,2,1,0:T(8,128)(2,1)} %get-tuple-element.14.rest_ref), custom_call_target="tpu_custom_call" | custom-call | tf_op jit(solution)/shard_map/edge/pallas_call | solution.py:345
  24.4 0.0 copy-start.2
  24.4 12.8 %all_to_all.10.x_ref = bf16[8,2,56,128]{3,2,1,0:T(8,128)(2,1)} all-to-all(bf16[8,2,56,128]{3,2,1,0:T(8,128)(2,1)} %edge.1), channel_id=1, replica_groups=mesh['tm'=8,'stn'=32] {'tm'}, dimensions={0} | all-to-all | bytes 458752 | tf_op jit(solution)/shard_map/all_to_all | solution.py:388
  37.2 2.5 %fine.1 = bf16[32,32,128]{2,1,0:T(8,128)(2,1)} custom-call(bf16[8,2,56,128]{3,2,1,0:T(8,128)(2,1)} %all_to_all.10.x_ref, bf16[2,448,512]{2,1,0:T(8,128)(2,1)} %constant.2.clone.table_ref), custom_call_target="tpu_custom_call" | custom-call | tf_op jit(solution)/shard_map/fine/pallas_call | solution.py:356
  39.7 11.4 %all-to-all-start.1 = ((bf16[32,16,2,128]{3,2,1,0:T(2,128)(2,1)}), bf16[32,16,2,128]{3,2,1,0:T(2,128)(2,1)S(1)}, u32[]{:S(2)}, u32[]{:S(2)}) async-start(bf16[32,16,2,128]{3,2,1,0:T(2,128)(2,1)} %bitcast.11), calls=%async_computation.1 | async-start | bytes 524288 | tf_op jit(solution)/shard_map/all_to_all | solution.py:391
  51.1 0.0 copy-done.2
  51.1 0.1 copy.12
  51.2 0.7 reshape.24.pairs_ref
  51.9 11.0 %all-to-all-done.1 = bf16[32,16,2,128]{3,2,1,0:T(2,128)(2,1)S(1)} async-done(((bf16[32,16,2,128]{3,2,1,0:T(2,128)(2,1)}), bf16[32,16,2,128]{3,2,1,0:T(2,128)(2,1)S(1)}, u32[]{:S(2)}, u32[]{:S(2)}) %all-to-all-start.1) | async-done | bytes 262176 | tf_op jit(solution)/shard_map/all_to_all | solution.py:391
  62.9 0.0 copy-start
  62.9 0.7 copy-done
  63.6 7.2 %pairs.1 = f32[1,36,2,128,128]{4,3,2,1,0:T(8,128)} custom-call(s32[512]{0:T(512)} %map_ref.1, s32[72]{0:T(128)} %reshape.24.pairs_ref, bf16[512,2,128]{2,1,0:T(2,128)(2,1)} %bitcast.10), custom_call_target="tpu_custom_call" | custom-call | tf_op jit(solution)/shard_map/pairs/pallas_call | solution.py:367
Async XLA Ops:
  12.0 9.5 %collective-permute-start = (f32[128,384]{1,0:T(8,128)}, f32[128,384]{1,0:T(8,128)S(1)}, u32[]{:S(2)}, u32[]{:S(2)}) collective-permute-start(f32[128,384]{1,0:T(8,128)} %get-tuple-element.10), channel_id=1, source_target_pairs={{0,32},{32,64},{64,96},{96,128},{128,160},{160,192},{192,224},{1,3... | collective-permute-start | bytes 589832 | tf_op jit(solution)/shard_map/ppermute | solution.py:385
  21.5 0.7 copy-start.1
  24.4 26.6 %copy-start.2 = (s32[36,2]{0,1:T(2,128)S(1)}, s32[36,2]{0,1:T(2,128)}, u32[]{:S(2)}) copy-start(s32[36,2]{0,1:T(2,128)} %param.12) | copy-start | bytes 868
  39.7 23.2 %all-to-all-start.1 = ((bf16[32,16,2,128]{3,2,1,0:T(2,128)(2,1)}), bf16[32,16,2,128]{3,2,1,0:T(2,128)(2,1)S(1)}, u32[]{:S(2)}, u32[]{:S(2)}) async-start(bf16[32,16,2,128]{3,2,1,0:T(2,128)(2,1)} %bitcast.11), calls=%async_computation.1 | async-start | bytes 524288 | tf_op jit(solution)/shard_map/all_to_all | solution.py:391
  62.9 0.7 copy-start
where the time goes:
time: 71.4 us; the launch traced here: 70.8 us
  Pallas kernels  24.4 us (34%)
  starting transfers between devices  13.1 us (18%)
  blocking collectives  12.8 us (18%)
  waiting for transfers between devices  11 us (15%)
  local copies, waits for them, and re-layouts  9.41 us (13%)
    all_to_all x1, blocking collectives, shards(): turned = lax.all_to_all(beamed, 'tm', 0, 0, tiled=True)  12.8 us
    all_to_all x1, starting transfers between devices, shards(): rows = lax.all_to_all(fine, 'stn', 0, 0, tiled=True)  11.4 us
    all_to_all x1, waiting for transfers between devices, shards(): rows = lax.all_to_all(fine, 'stn', 0, 0, tiled=True)  11 us
    pallas_call x1, Pallas kernels, main_call(): pl.pallas_call(main_kernel, out_shape=(jax.ShapeDtypeStruct((128, EDGE *...  7.73 us
    pallas_call x1, Pallas kernels, pairs_call(): pl.pallas_call(pairs_kernel, grid=(tiles // PER_STEP,), out_shape=jax.Sha...  7.22 us
    pallas_call x1, Pallas kernels, halo_call(): pl.pallas_call(halo_kernel, out_shape=(jax.ShapeDtypeStruct((256, FRAME),...  4.74 us
    reshape x1, local copies, waits for them, and re-layouts, shards(): x = voltages.reshape(stations, 2, LOCAL * COLS, 128).transpose(0, 2, 1, 3)  3.64 us
    pallas_call x1, Pallas kernels, fine_call(): pl.pallas_call(fine_kernel, out_shape=jax.ShapeDtypeStruct((32, SIGS, 128...  2.5 us
  transfers between devices with their start and end apart: 2, of which 1 were waited for; matrix products, arithmetic and copies ran while one was open for 1% of the time, Pallas kernels for 11%

commit v1 on v0

v1 whole, which is shorter than its diff:
```python
import functools
import math

import jax
import jax.numpy as jnp
import numpy as np
from jax import lax
from jax.experimental import pallas as pl
from jax.experimental.pallas import tpu as pltpu
from jax.sharding import PartitionSpec as P

GROUP = 54
BLOCK = 128
TAPS = 12
FRAME = 768
COLS = FRAME // 128
LOCAL = 27
EDGE = 12
SIGS = 32
KEPT = 64
ROWS = 56

F32 = jnp.float32
BF16 = jnp.bfloat16
NT = (((1,), (1,)), ((), ()))
NN = (((1,), (0,)), ((), ()))


def vmem():
    return pl.BlockSpec(memory_space=pltpu.VMEM)


def anywhere():
    return pl.BlockSpec(memory_space=pltpu.HBM)


def smem():
    return pl.BlockSpec(memory_space=pltpu.SMEM)


def granted(mebibytes):
    return pltpu.CompilerParams(vmem_limit_bytes=mebibytes * 2**20)


def split(value):
    high = value.astype(BF16)
    return high, (value - high.astype(F32)).astype(BF16)


def turn(phase):
    quarter = jnp.floor((phase + 96.0) * (1.0 / 192.0))
    angle = (phase - quarter * 192.0) * (2.0 * math.pi / FRAME)
    square = angle * angle
    sine = 1.0 / 362880.0
    for term in (-1.0 / 5040.0, 1.0 / 120.0, -1.0 / 6.0, 1.0):
        sine = sine * square + term
    sine = sine * angle
    cosine = 1.0 / 40320.0
    for term in (-1.0 / 720.0, 1.0 / 24.0, -0.5, 1.0):
        cosine = cosine * square + term
    quarter = quarter.astype(jnp.int32) & 3
    odd = (quarter & 1) == 1
    first = jnp.where(odd, sine, cosine)
    second = jnp.where(odd, cosine, sine)
    flip = (quarter == 1) | (quarter == 2)
    return jnp.where(flip, -first, first), jnp.where(quarter >= 2, second, -second)


def coarse_table(kept_ref, turned_ref, w_ref):
    turned_ref[...] = jnp.broadcast_to(kept_ref[...].astype(F32), (128, KEPT)).T
    lane = lax.broadcasted_iota(jnp.int32, (8, 128), 1).astype(F32)
    factor = 1.0 / math.sqrt(FRAME)
    for j in range(4):
        for h in range(2):
            kept = turned_ref[pl.ds(4 * h + j, 8, stride=8), :]
            re, im = turn(kept * lane)
            re, im = re * factor, im * factor
            step_re, step_im = turn(kept * 128.0)
            row = (j * 2 + h) * 8
            for col in range(COLS):
                span = slice(col * 128, col * 128 + 128)
                for part, value in enumerate((re, im)):
                    high, low = split(value)
                    w_ref[part * KEPT + row : part * KEPT + row + 8, span] = high
                    w_ref[128 + part * KEPT + row : 128 + part * KEPT + row + 8, span] = low
                re, im = re * step_re - im * step_im, re * step_im + im * step_re


def filter_column(x_ref, proto_ref, high_ref, low_ref, col, half, lane_at, first, count, outputs):
    taken = pl.ds(pl.multiple_of(col * 128, 128), 128)
    put = pl.ds(pl.multiple_of(lane_at * 128, 128), 128)
    side = pl.ds(pl.multiple_of(half * 16, 16), 16)
    taps = [jnp.broadcast_to(proto_ref[k : k + 1, taken], (16, 128)) for k in range(TAPS)]
    sums, left = {}, {}
    for out in outputs.values():
        left[out] = left.get(out, 0) + 1
    for n in range(count):
        x = x_ref[(first + n) * COLS + col, side, :].astype(F32)
        for k in range(TAPS):
            if (k, n) not in outputs:
                continue
            out = outputs[k, n]
            sums[out] = sums[out] + taps[k] * x if out in sums else taps[k] * x
            left[out] -= 1
            if left[out] == 0:
                high, low = split(sums.pop(out))
                rows = pl.ds(pl.multiple_of(out * SIGS + half * 16, 16), 16)
                high_ref[rows, put] = high
                low_ref[rows, put] = low


def coarse_sums(x_ref, proto_ref, w_ref, highs, lows, sums_ref, first, count, outputs, chunk):
    def transform(pair, q):
        rows = pl.ds(pl.multiple_of(q * chunk, chunk), chunk)
        span = slice(pair * 256, pair * 256 + 256)
        both = lax.dot_general(
            w_ref[:, span], highs[pair][rows, :], NT, preferred_element_type=F32
        )
        rest = lax.dot_general(
            w_ref[:128, span], lows[pair][rows, :], NT, preferred_element_type=F32
        )
        value = both[:128] + both[128:] + rest
        if pair > 0:
            value = value + sums_ref[:, rows]
        sums_ref[:, rows] = value

    for pair in range(COLS // 2):

        @pl.loop(0, 4)
        def _(q):
            if pair > 0:
                transform(pair - 1, q)
            filter_column(
                x_ref, proto_ref, highs[pair], lows[pair],
                pair * 2 + q // 2, q % 2, q // 2, first, count, outputs,
            )

    for q in range(4):
        transform(COLS // 2 - 1, q)


def beam_and_deal(load, jones_ref, dealt_ref, tiles, tile_at, stride):
    lane = lax.broadcasted_iota(jnp.int32, (8, 128), 1)
    even = lane % 2 == 0
    low_half = lane < 64
    even_chunk = (lane // 32) % 2 == 0

    def swap(value):
        return jnp.where(even, pltpu.roll(value, 127, 1), pltpu.roll(value, 1, 1))

    def beam(tile, row):
        re, im = load(row, tile), load(KEPT + row, tile)
        swap_re, swap_im = swap(re), swap(im)
        own_re, own_im, cross_re, cross_im = (
            jones_ref[n * KEPT + row : n * KEPT + row + 8, :] for n in range(4)
        )
        return (
            own_re * re - own_im * im + cross_re * swap_re - cross_im * swap_im,
            own_re * im + own_im * re + cross_re * swap_im + cross_im * swap_re,
        )

    for tile in range(tiles):
        for h in range(2):
            beams = [beam(tile, (j * 2 + h) * 8) for j in range(4)]
            for part in range(2):
                v = [beams[j][part] for j in range(4)]
                u = [None] * 4
                for j in range(2):
                    u[j] = jnp.where(low_half, v[j], pltpu.roll(v[j + 2], 64, 1))
                    u[j + 2] = jnp.where(low_half, pltpu.roll(v[j], 64, 1), v[j + 2])
                for i in (0, 2):
                    first = jnp.where(even_chunk, u[i], pltpu.roll(u[i + 1], 32, 1))
                    second = jnp.where(even_chunk, pltpu.roll(u[i], 96, 1), u[i + 1])
                    for n, value in enumerate((first, second)):
                        frame = (tile_at + tile) * 4 + i + n
                        row = h * (stride // 2) + (frame - tile_at * 4) * 2 + part
                        dealt_ref[pl.ds(row, 8, stride=stride), :] = value


MAIN_OUT = {
    (k, n): n + TAPS - 1 - k
    for n in range(LOCAL)
    for k in range(TAPS)
    if n + TAPS - 1 - k < LOCAL
}


def halo_outputs():
    return {(k, f + k): f for f in range(11) for k in range(TAPS) if f + k <= 10}


def clear(refs, first):
    for ref in refs:
        ref[first : first + SIGS, :] = jnp.zeros((SIGS, 256), BF16)


def halo_kernel(
    x_ref, proto_in, kept_in, beam_in, w_ref, out_ref, xt_ref, proto_ref, beam_ref,
    kept_ref, turned_ref, sums_ref, h0, h1, h2, l0, l1, l2, sems, more,
):
    def rows_of(s, first, count, sem):
        tiles = pl.ds(first * COLS, count * COLS)
        return pltpu.make_async_copy(x_ref.at[s, tiles], xt_ref.at[tiles, pl.ds(2 * s, 2)], sem)

    stations = x_ref.shape[0]
    late = [rows_of(s, LOCAL - 11, 11, sems.at[0, s]) for s in range(stations)]
    early = [rows_of(s, 0, LOCAL - 11, sems.at[1, s]) for s in range(stations)]
    kept_copy = pltpu.make_async_copy(kept_in, kept_ref, more.at[0])
    proto_copy = pltpu.make_async_copy(proto_in, proto_ref, more.at[1])
    beam_copy = pltpu.make_async_copy(beam_in, beam_ref, more.at[2])
    for copy in [kept_copy, proto_copy] + late + early + [beam_copy]:
        copy.start()
    clear((h0, h1, h2, l0, l1, l2), 11 * SIGS)
    kept_copy.wait()
    coarse_table(kept_ref, turned_ref, w_ref)
    for copy in [proto_copy] + late:
        copy.wait()
    coarse_sums(
        xt_ref, proto_ref, w_ref, (h0, h1, h2), (l0, l1, l2), sums_ref,
        LOCAL - 11, 11, halo_outputs(), 128,
    )
    out_ref[...] = sums_ref[:, : EDGE * SIGS]
    for copy in early + [beam_copy]:
        copy.wait()


def main_kernel(
    xt_ref, proto_ref, w_ref, beam_ref, sums_ref, jones_ref, out_ref,
    h0, h1, h2, l0, l1, l2, dealt_ref, turned_ref,
):
    side = lax.broadcasted_iota(jnp.int32, (8, 128), 1) % 2 == 0
    for part in range(2):
        for q in range(2):
            rows = beam_ref[pl.ds(q * 2 + part, SIGS, stride=4), :]
            wide = jnp.concatenate([rows.T] * 4, axis=1)
            turned_ref[q * KEPT : q * KEPT + KEPT, :] = wide
        for j in range(4):
            for h in range(2):
                first = turned_ref[pl.ds(4 * h + j, 8, stride=8), :]
                second = turned_ref[pl.ds(KEPT + 4 * h + j, 8, stride=8), :]
                row = (j * 2 + h) * 8
                own = jnp.where(side, first, second)
                cross = jnp.where(side, second, first)
                jones_ref[part * KEPT + row : part * KEPT + row + 8, :] = own
                jones_ref[(2 + part) * KEPT + row : (2 + part) * KEPT + row + 8, :] = cross
    clear((h0, h1, h2, l0, l1, l2), LOCAL * SIGS)
    coarse_sums(
        xt_ref, proto_ref, w_ref, (h0, h1, h2), (l0, l1, l2), sums_ref,
        0, LOCAL, MAIN_OUT, 256,
    )
    beam_and_deal(
        lambda row, tile: sums_ref[row : row + 8, (3 + tile) * 128 : (3 + tile) * 128 + 128],
        jones_ref, dealt_ref, 4, 3, 64,
    )
    for d in range(8):
        for h in range(2):
            out_ref[d, h] = dealt_ref[d * 64 + h * 32 : d * 64 + h * 32 + 32, :].astype(BF16)


def edge_kernel(halo_ref, edge_ref, jones_ref, rest_ref, out_ref, dealt_ref):
    def load(row, tile):
        span = slice(tile * 128, tile * 128 + 128)
        return halo_ref[row : row + 8, span] + edge_ref[row : row + 8, span]

    beam_and_deal(load, jones_ref, dealt_ref, 3, 0, 48)
    for d in range(8):
        for h in range(2):
            out_ref[d, h, 0:24, :] = dealt_ref[d * 48 + h * 24 : d * 48 + h * 24 + 24, :].astype(BF16)
            out_ref[d, h, 24:56, :] = rest_ref[d, h]


def fine_table():
    blocks, frames = 8, LOCAL
    length = blocks * frames
    k = np.arange(length)
    angle = 2.0 * np.pi * ((k[:, None] * k[None, :]) % length) / length
    cosine = np.cos(angle) / np.sqrt(length)
    sine = np.sin(angle) / np.sqrt(length)
    groups = length // GROUP
    table = np.zeros((blocks, ROWS, groups, 128))
    view = table[:, : 2 * frames].reshape(blocks, frames, 2, groups, 128)
    cosine = cosine.reshape(blocks, frames, groups, GROUP)
    sine = sine.reshape(blocks, frames, groups, GROUP)
    view[:, :, 0, :, :GROUP] = cosine
    view[:, :, 1, :, :GROUP] = sine
    view[:, :, 0, :, GROUP : 2 * GROUP] = -sine
    view[:, :, 1, :, GROUP : 2 * GROUP] = cosine
    table[:, : 2 * frames] = view.reshape(blocks, 2 * frames, groups, 128)
    table = table.reshape(blocks * ROWS, groups * 128).astype(np.float32)
    high = table.astype(jnp.bfloat16)
    low = (table - high.astype(np.float32)).astype(jnp.bfloat16)
    return np.stack([high, low])


def fine_kernel(x_ref, table_ref, out_ref):
    for h in range(2):
        rows = x_ref[:, h].astype(F32).reshape(8 * ROWS, 128)
        turned = rows.T.astype(BF16)
        fine = lax.dot_general(turned, table_ref[0], NN, preferred_element_type=F32)
        fine = fine + lax.dot_general(turned, table_ref[1], NN, preferred_element_type=F32)
        for j in range(4):
            for g in range(4):
                piece = fine[j * 32 : j * 32 + 32, g * 128 : g * 128 + 128]
                out_ref[(h * 4 + j) * 4 + g] = piece.astype(BF16)


def pairs_kernel(map_ref, pairs_ref, x_ref, out_ref, ordered_ref, own_ref, turned_ref, made, sems):
    tiles = made.shape[0]
    rows = ordered_ref.reshape(1024, 128)

    @pl.loop(0, 512, unroll=8)
    def _(row):
        ordered_ref[map_ref[row]] = x_ref[row]

    lane = lax.broadcasted_iota(jnp.int32, (128, 128), 1)
    for block in range(8):
        span = slice(block * 128, block * 128 + 128)
        own = rows[span, :]
        own_ref[span, :] = own
        value = own.astype(F32)
        turned = jnp.where(
            lane < GROUP, -pltpu.roll(value, 128 - GROUP, 1), pltpu.roll(value, GROUP, 1)
        )
        turned_ref[span, :] = turned.astype(BF16)

    def send(tile):
        return pltpu.make_async_copy(made.at[tile], out_ref.at[0, tile], sems.at[tile])

    @pl.loop(0, tiles, unroll=12)
    def _(tile):
        left = pl.ds(pl.multiple_of(pairs_ref[0, tile] * 128, 128), 128)
        right = pl.ds(pl.multiple_of(pairs_ref[1, tile] * 128, 128), 128)
        other = jnp.concatenate([own_ref[right, :], turned_ref[right, :]], axis=0)
        product = lax.dot_general(own_ref[left, :], other, NT, preferred_element_type=F32)
        product = product * (1.0 / GROUP)
        made[tile, 0] = product[:, :128]
        made[tile, 1] = product[:, 128:]
        send(tile).start()

    @pl.loop(0, tiles)
    def _(tile):
        send(tile).wait()


def columns(rows):
    return [pltpu.VMEM((rows, 256), BF16)] * 6


def halo_call(x, proto, kept, beam):
    return pl.pallas_call(
        halo_kernel,
        out_shape=(
            jax.ShapeDtypeStruct((256, FRAME), BF16),
            jax.ShapeDtypeStruct((128, EDGE * SIGS), F32),
            jax.ShapeDtypeStruct((LOCAL * COLS, SIGS, 128), BF16),
            jax.ShapeDtypeStruct(proto.shape, F32),
            jax.ShapeDtypeStruct(beam.shape, F32),
        ),
        in_specs=[anywhere()] * 4,
        out_specs=(vmem(),) * 5,
        scratch_shapes=[
            pltpu.VMEM((1, KEPT), jnp.int32),
            pltpu.VMEM((KEPT, 128), F32),
            pltpu.VMEM((128, 512), F32),
            *columns(512),
            pltpu.SemaphoreType.DMA((2, 16)),
            pltpu.SemaphoreType.DMA((3,)),
        ],
        compiler_params=granted(8),
        name="halo",
    )(x, proto, kept, beam)


def main_call(xt, proto, table, beam):
    return pl.pallas_call(
        main_kernel,
        out_shape=(
            jax.ShapeDtypeStruct((128, 1024), F32),
            jax.ShapeDtypeStruct((4 * KEPT, 128), F32),
            jax.ShapeDtypeStruct((8, 2, 32, 128), BF16),
        ),
        in_specs=[vmem()] * 4,
        out_specs=(vmem(),) * 3,
        scratch_shapes=[
            *columns(1024),
            pltpu.VMEM((8 * 64, 128), F32),
            pltpu.VMEM((2 * KEPT, 128), F32),
        ],
        compiler_params=granted(14),
        cost_estimate=pl.CostEstimate(flops=10**9, bytes_accessed=4 * 10**6, transcendentals=0),
        name="main",
    )(xt, proto, table, beam)


def edge_call(halo, edge, jones, rest):
    return pl.pallas_call(
        edge_kernel,
        out_shape=jax.ShapeDtypeStruct((8, 2, ROWS, 128), BF16),
        in_specs=[vmem()] * 4,
        out_specs=vmem(),
        scratch_shapes=[pltpu.VMEM((8 * 48, 128), F32)],
        compiler_params=granted(4),
        name="edge",
    )(halo, edge, jones, rest)


def fine_call(turned, table):
    return pl.pallas_call(
        fine_kernel,
        out_shape=jax.ShapeDtypeStruct((32, SIGS, 128), BF16),
        in_specs=[vmem()] * 2,
        out_specs=vmem(),
        compiler_params=granted(8),
        name="fine",
    )(turned, table)


def pairs_call(station_map, tile_pairs, rows):
    tiles = tile_pairs.shape[1]
    return pl.pallas_call(
        pairs_kernel,
        out_shape=jax.ShapeDtypeStruct((1, tiles, 2, BLOCK, BLOCK), F32),
        in_specs=[smem(), smem(), vmem()],
        out_specs=anywhere(),
        scratch_shapes=[
            pltpu.VMEM((512, 2, 128), BF16),
            pltpu.VMEM((1024, 128), BF16),
            pltpu.VMEM((1024, 128), BF16),
            pltpu.VMEM((tiles, 2, BLOCK, BLOCK), F32),
            pltpu.SemaphoreType.DMA((tiles,)),
        ],
        compiler_params=granted(10),
        name="pairs",
    )(station_map, tile_pairs, rows)


def kept_in_hbm(value):
    return pltpu.with_memory_space_constraint(value, pltpu.HBM)


def shards(voltages, prototype, kept_channels, beam_jones, station_map, tile_pairs):
    stations = voltages.shape[0]
    x = voltages.reshape(stations, 2, LOCAL * COLS, 128).transpose(0, 2, 1, 3)
    table, halo, xt, proto, beam = halo_call(
        kept_in_hbm(x),
        kept_in_hbm(prototype),
        kept_in_hbm(kept_channels.reshape(1, KEPT)),
        kept_in_hbm(beam_jones.reshape(128, KEPT)),
    )
    blocks = lax.axis_size("tm")
    halo = lax.ppermute(halo, "tm", [(n, n + 1) for n in range(blocks - 1)])
    sums, jones, rest = main_call(xt, proto, table, beam)
    beamed = edge_call(halo, sums, jones, rest)
    turned = lax.all_to_all(beamed, "tm", 0, 0, tiled=True)
    fine = fine_call(turned, jnp.asarray(fine_table()))
    fine = fine.reshape(32, 16, 2, 128)
    rows = lax.all_to_all(fine, "stn", 0, 0, tiled=True)
    return pairs_call(station_map, tile_pairs.T, rows.reshape(512, 2, 128))


def solution(mesh):
    placed = (P("stn", None, "tm"), P(), P(), P("stn", None, None, None, None), P(), P())
    return jax.shard_map(
        shards,
        mesh=mesh,
        in_specs=placed,
        out_specs=P(("tm", "stn"), None, None, None, None),
        check_vma=False,
    )
```

time: 71.4 us -> 50.8 us (0.71)
  blocking collectives: 12.8 us -> 35.4 us
  starting transfers between devices: 13.1 us -> 1.75 us
  Pallas kernels: 24.4 us -> 13.4 us
  waiting for transfers between devices: 11 us -> 0.01 us
  local copies, waits for them, and re-layouts: 9.41 us -> 0.02 us
    all_to_all x0 -> x1, blocking collectives: none -> 22.9 us  [shards(): rows = lax.all_to_all(fine, 'stn', 0, 0, tiled=True)]
    all_to_all x1 -> x0, starting transfers between devices: 11.4 us -> none  [shards(): rows = lax.all_to_all(fine, 'stn', 0, 0, tiled=True)]
    all_to_all x1 -> x0, waiting for transfers between devices: 11 us -> none  [shards(): rows = lax.all_to_all(fine, 'stn', 0, 0, tiled=True)]
    pallas_call x2, Pallas kernels: 15 us -> 8.28 us  [the longest x1 4.24 us: pairs_call(): pl.pallas_call(pairs_kernel, out_shape=jax.ShapeDtypeStruct((1, tiles, 2,...]
    reshape x4 -> x0, local copies, waits for them, and re-layouts: 5.77 us -> none  [the longest x1 3.64 us: shards(): x = voltages.reshape(stations, 2, LOCAL * COLS, 128).transpose(0, 2, 1, 3)]
    transpose x2 -> x0, local copies, waits for them, and re-layouts: 2.18 us -> none  [the longest x1 2.09 us: shards(): x = voltages.reshape(stations, 2, LOCAL * COLS, 128).transpose(0, 2, 1, 3)]
    pallas_call x1, Pallas kernels: 2.5 us -> 0.49 us  [fine_call(): pl.pallas_call(fine_kernel, out_shape=jax.ShapeDtypeStruct((32, SIGS, 128...]
    pallas_call x1, Pallas kernels: 2.24 us -> 0.4 us  [edge_call(): pl.pallas_call(edge_kernel, out_shape=jax.ShapeDtypeStruct((8, 2, ROWS, 1...]
  transfers between devices with their start and end apart: 2 -> 1, of which waited for: 1 -> 0; matrix products, arithmetic and copies ran while one was open for 1% -> 0% of each run, Pallas kernels for 11% -> 8%
where the time goes in v1:
time: 50.8 us; the launch traced here: 50.6 us
  blocking collectives  35.4 us (70%)
  Pallas kernels  13.4 us (26%)
  starting transfers between devices  1.75 us (3%)
    all_to_all x1, blocking collectives, shards(): rows = lax.all_to_all(fine, 'stn', 0, 0, tiled=True)  22.9 us
    all_to_all x1, blocking collectives, shards(): turned = lax.all_to_all(beamed, 'tm', 0, 0, tiled=True)  12.4 us
    pallas_call x1, Pallas kernels, pairs_call(): pl.pallas_call(pairs_kernel, out_shape=jax.ShapeDtypeStruct((1, tiles, 2,...  4.24 us
    pallas_call x1, Pallas kernels, halo_call(): pl.pallas_call(halo_kernel, out_shape=(jax.ShapeDtypeStruct((256, FRAME),...  4.19 us
    pallas_call x1, Pallas kernels, main_call(): pl.pallas_call(main_kernel, out_shape=(jax.ShapeDtypeStruct((128, 1024),...  4.04 us
    ppermute x1, starting transfers between devices, shards(): halo = lax.ppermute(halo, 'tm', [(n, n + 1) for n in range(blocks - 1)])  1.75 us
  transfers between devices with their start and end apart: 1, of which 0 were waited for; matrix products, arithmetic and copies ran while one was open for 0% of the time, Pallas kernels for 8%

profile of v1, /device:TPU:32, one launch (start us, length us, event | category | flops | bytes accessed | tf_op | source)
XLA Modules:
  0.0 50.6 jit_solution(9380307529410282924)
XLA Ops:
  0.0 4.2 %halo.1 = (bf16[256,768]{1,0:T(8,128)(2,1)S(1)}, f32[128,384]{1,0:T(8,128)S(1)}, bf16[162,32,128]{2,1,0:T(8,128)(2,1)S(1)}, f32[12,768]{1,0:T(8,128)S(1)}, f32[128,64]{1,0:T(8,128)S(1)}) custom-call(bf16[16,162,2,128]{3,2,1,0:T(2,128)(2,1)} %bitcast.11, f32[12,768]{1,0:T(8,128)} %proto_in.1, s32[1,64]{1,0:T(1,128)} %bitcast.13, f32[128,64]{1,0:T(8,128)} %bitcast.12), custom_call_target="tpu_custom_call" | custom-call | tf_op jit(solution)/shard_map/halo/pallas_call | solution.py:350
  4.2 1.8 %collective-permute-start = (f32[128,384]{1,0:T(8,128)S(1)}, f32[128,384]{1,0:T(8,128)S(1)}, u32[]{:S(2)}, u32[]{:S(2)}) collective-permute-start(f32[128,384]{1,0:T(8,128)S(1)} %get-tuple-element.13), channel_id=1, source_target_pairs={{0,32},{32,64},{64,96},{96,128},{128,160},{160,192},{192,224},{1,3... | collective-permute-start | bytes 589832 | tf_op jit(solution)/shard_map/ppermute | solution.py:451
  6.0 4.0 %main.1 = (f32[128,1024]{1,0:T(8,128)S(1)}, f32[256,128]{1,0:T(8,128)S(1)}, bf16[8,2,32,128]{3,2,1,0:T(8,128)(2,1)S(1)}) custom-call(bf16[162,32,128]{2,1,0:T(8,128)(2,1)S(1)} %get-tuple-element.14.xt_ref, f32[12,768]{1,0:T(8,128)S(1)} %get-tuple-element.15.proto_ref, bf16[256,768]{1,0:T(8,128)(2,1)S(1)} %get-tuple-element.16.w_ref, ...), custom_call_target="tpu_custom_call" | custom-call | flops 1000000000 | bytes 4000000 | tf_op jit(solution)/shard_map/main/pallas_call | solution.py:375
  10.0 0.0 copy-start
  10.0 0.0 collective-permute-done.halo_ref
  10.0 0.4 edge.1
  10.4 0.0 copy-start.1
  10.4 0.0 copy-start.2
  10.5 12.4 %all_to_all.10.x_ref = bf16[8,2,56,128]{3,2,1,0:T(8,128)(2,1)S(1)} all-to-all(bf16[8,2,56,128]{3,2,1,0:T(8,128)(2,1)S(1)} %edge.1), channel_id=1, replica_groups=mesh['tm'=8,'stn'=32] {'tm'}, dimensions={0} | all-to-all | bytes 458752 | tf_op jit(solution)/shard_map/all_to_all | solution.py:454
  22.9 0.0 copy-done
  22.9 0.5 fine.1
  23.4 22.9 %all_to_all.11 = bf16[32,16,2,128]{3,2,1,0:T(2,128)(2,1)S(1)} all-to-all(bf16[32,16,2,128]{3,2,1,0:T(2,128)(2,1)S(1)} %bitcast.9), channel_id=1, replica_groups=mesh['tm'=8,'stn'=32] {'stn'}, dimensions={0} | all-to-all | bytes 524288 | tf_op jit(solution)/shard_map/all_to_all | solution.py:457
  46.3 0.0 copy-done.1
  46.3 0.0 copy-done.2
  46.3 4.2 %pairs.1 = f32[1,36,2,128,128]{4,3,2,1,0:T(8,128)} custom-call(s32[512]{0:T(512)S(1)} %copy-done.1, s32[2,36]{1,0:T(2,128)S(1)} %bitcast.10, bf16[512,2,128]{2,1,0:T(2,128)(2,1)S(1)} %bitcast.8), custom_call_target="tpu_custom_call" | custom-call | tf_op jit(solution)/shard_map/pairs/pallas_call | solution.py:420
Async XLA Ops:
  4.2 5.8 %collective-permute-start = (f32[128,384]{1,0:T(8,128)S(1)}, f32[128,384]{1,0:T(8,128)S(1)}, u32[]{:S(2)}, u32[]{:S(2)}) collective-permute-start(f32[128,384]{1,0:T(8,128)S(1)} %get-tuple-element.13), channel_id=1, source_target_pairs={{0,32},{32,64},{64,96},{96,128},{128,160},{160,192},{192,224},{1,3... | collective-permute-start | bytes 589832 | tf_op jit(solution)/shard_map/ppermute | solution.py:451
  10.0 12.9 %copy-start = (bf16[2,448,512]{2,1,0:T(8,128)(2,1)S(1)}, bf16[2,448,512]{2,1,0:T(8,128)(2,1)}, u32[]{:S(2)}) copy-start(bf16[2,448,512]{2,1,0:T(8,128)(2,1)} %constant.2.clone.table_ref) | copy-start | bytes 2752516
  10.4 35.9 %copy-start.1 = (s32[512]{0:T(512)S(1)}, s32[512]{0:T(512)}, u32[]{:S(2)}) copy-start(s32[512]{0:T(512)} %map_ref.1) | copy-start | bytes 6148
  10.4 35.9 %copy-start.2 = (s32[36,2]{0,1:T(2,128)S(1)}, s32[36,2]{0,1:T(2,128)}, u32[]{:S(2)}) copy-start(s32[36,2]{0,1:T(2,128)} %param.12) | copy-start | bytes 868

commit v2 on v1

--- a/solution.py
+++ b/solution.py
@@ -15,10 +15,12 @@
 FRAME = 768
 COLS = FRAME // 128
 LOCAL = 27
-EDGE = 12
+SPREAD = LOCAL + TAPS - 1
+TILES = 10
+STEPS = 5
 SIGS = 32
 KEPT = 64
-ROWS = 56
+ROWS = 80
 
 F32 = jnp.float32
 BF16 = jnp.bfloat16
@@ -67,7 +69,7 @@
 
 
 def coarse_table(kept_ref, turned_ref, w_ref):
-    turned_ref[...] = jnp.broadcast_to(kept_ref[...].astype(F32), (128, KEPT)).T
+    turned_ref[:KEPT, :] = jnp.broadcast_to(kept_ref[...].astype(F32), (128, KEPT)).T
     lane = lax.broadcasted_iota(jnp.int32, (8, 128), 1).astype(F32)
     factor = 1.0 / math.sqrt(FRAME)
     for j in range(4):
@@ -86,7 +88,7 @@
                 re, im = re * step_re - im * step_im, re * step_im + im * step_re
 
 
-def filter_column(x_ref, proto_ref, high_ref, low_ref, col, half, lane_at, first, count, outputs):
+def filter_column(x_ref, proto_ref, high_ref, low_ref, col, half, lane_at, outputs):
     taken = pl.ds(pl.multiple_of(col * 128, 128), 128)
     put = pl.ds(pl.multiple_of(lane_at * 128, 128), 128)
     side = pl.ds(pl.multiple_of(half * 16, 16), 16)
@@ -94,8 +96,8 @@
     sums, left = {}, {}
     for out in outputs.values():
         left[out] = left.get(out, 0) + 1
-    for n in range(count):
-        x = x_ref[(first + n) * COLS + col, side, :].astype(F32)
+    for n in range(LOCAL):
+        x = x_ref[n * COLS + col, side, :].astype(F32)
         for k in range(TAPS):
             if (k, n) not in outputs:
                 continue
@@ -109,7 +111,9 @@
                 low_ref[rows, put] = low
 
 
-def coarse_sums(x_ref, proto_ref, w_ref, highs, lows, sums_ref, first, count, outputs, chunk):
+def coarse_sums(x_ref, proto_ref, w_ref, highs, lows, sums_ref, outputs):
+    chunk = TILES * 128 // STEPS
+
     def transform(pair, q):
         rows = pl.ds(pl.multiple_of(q * chunk, chunk), chunk)
         span = slice(pair * 256, pair * 256 + 256)
@@ -126,20 +130,23 @@
 
     for pair in range(COLS // 2):
 
+        if pair > 0:
+            transform(pair - 1, STEPS - 1)
+
         @pl.loop(0, 4)
         def _(q):
             if pair > 0:
                 transform(pair - 1, q)
             filter_column(
                 x_ref, proto_ref, highs[pair], lows[pair],
-                pair * 2 + q // 2, q % 2, q // 2, first, count, outputs,
+                pair * 2 + q // 2, q % 2, q // 2, outputs,
             )
 
-    for q in range(4):
+    for q in range(STEPS):
         transform(COLS // 2 - 1, q)
 
 
-def beam_and_deal(load, jones_ref, dealt_ref, tiles, tile_at, stride):
+def beam_and_deal(load, jones_ref, dealt_ref, tiles, stride):
     lane = lax.broadcasted_iota(jnp.int32, (8, 128), 1)
     even = lane % 2 == 0
     low_half = lane < 64
@@ -172,8 +179,7 @@
                     first = jnp.where(even_chunk, u[i], pltpu.roll(u[i + 1], 32, 1))
                     second = jnp.where(even_chunk, pltpu.roll(u[i], 96, 1), u[i + 1])
                     for n, value in enumerate((first, second)):
-                        frame = (tile_at + tile) * 4 + i + n
-                        row = h * (stride // 2) + (frame - tile_at * 4) * 2 + part
+                        row = h * (stride // 2) + (tile * 4 + i + n) * 2 + part
                         dealt_ref[pl.ds(row, 8, stride=stride), :] = value
 
 
@@ -185,49 +191,12 @@
 }
 
 
-def halo_outputs():
-    return {(k, f + k): f for f in range(11) for k in range(TAPS) if f + k <= 10}
-
-
-def clear(refs, first):
+def clear(refs, first, last):
     for ref in refs:
-        ref[first : first + SIGS, :] = jnp.zeros((SIGS, 256), BF16)
-
-
-def halo_kernel(
-    x_ref, proto_in, kept_in, beam_in, w_ref, out_ref, xt_ref, proto_ref, beam_ref,
-    kept_ref, turned_ref, sums_ref, h0, h1, h2, l0, l1, l2, sems, more,
-):
-    def rows_of(s, first, count, sem):
-        tiles = pl.ds(first * COLS, count * COLS)
-        return pltpu.make_async_copy(x_ref.at[s, tiles], xt_ref.at[tiles, pl.ds(2 * s, 2)], sem)
-
-    stations = x_ref.shape[0]
-    late = [rows_of(s, LOCAL - 11, 11, sems.at[0, s]) for s in range(stations)]
-    early = [rows_of(s, 0, LOCAL - 11, sems.at[1, s]) for s in range(stations)]
-    kept_copy = pltpu.make_async_copy(kept_in, kept_ref, more.at[0])
-    proto_copy = pltpu.make_async_copy(proto_in, proto_ref, more.at[1])
-    beam_copy = pltpu.make_async_copy(beam_in, beam_ref, more.at[2])
-    for copy in [kept_copy, proto_copy] + late + early + [beam_copy]:
-        copy.start()
-    clear((h0, h1, h2, l0, l1, l2), 11 * SIGS)
-    kept_copy.wait()
-    coarse_table(kept_ref, turned_ref, w_ref)
-    for copy in [proto_copy] + late:
-        copy.wait()
-    coarse_sums(
-        xt_ref, proto_ref, w_ref, (h0, h1, h2), (l0, l1, l2), sums_ref,
-        LOCAL - 11, 11, halo_outputs(), 128,
-    )
-    out_ref[...] = sums_ref[:, : EDGE * SIGS]
-    for copy in early + [beam_copy]:
-        copy.wait()
-
-
-def main_kernel(
-    xt_ref, proto_ref, w_ref, beam_ref, sums_ref, jones_ref, out_ref,
-    h0, h1, h2, l0, l1, l2, dealt_ref, turned_ref,
-):
+        ref[first:last, :] = jnp.zeros((last - first, 256), BF16)
+
+
+def deal_beam(beam_ref, turned_ref, jones_ref):
     side = lax.broadcasted_iota(jnp.int32, (8, 128), 1) % 2 == 0
     for part in range(2):
         for q in range(2):
@@ -243,49 +212,61 @@
                 cross = jnp.where(side, second, first)
                 jones_ref[part * KEPT + row : part * KEPT + row + 8, :] = own
                 jones_ref[(2 + part) * KEPT + row : (2 + part) * KEPT + row + 8, :] = cross
-    clear((h0, h1, h2, l0, l1, l2), LOCAL * SIGS)
+
+
+def front_kernel(
+    x_ref, proto_in, kept_in, beam_in, out_ref, xt_ref, proto_ref, beam_ref, kept_ref,
+    w_ref, jones_ref, turned_ref, sums_ref, dealt_ref, h0, h1, h2, l0, l1, l2, sems, more,
+):
+    stations = x_ref.shape[0]
+    rows = [
+        pltpu.make_async_copy(x_ref.at[s], xt_ref.at[:, pl.ds(2 * s, 2)], sems.at[s])
+        for s in range(stations)
+    ]
+    kept_copy = pltpu.make_async_copy(kept_in, kept_ref, more.at[0])
+    proto_copy = pltpu.make_async_copy(proto_in, proto_ref, more.at[1])
+    beam_copy = pltpu.make_async_copy(beam_in, beam_ref, more.at[2])
+    for copy in [kept_copy, beam_copy, proto_copy] + rows:
+        copy.start()
+    clear((h0, h1, h2, l0, l1, l2), SPREAD * SIGS, TILES * 128)
+    kept_copy.wait()
+    beam_copy.wait()
+    coarse_table(kept_ref, turned_ref, w_ref)
+    deal_beam(beam_ref, turned_ref, jones_ref)
+    for copy in [proto_copy] + rows:
+        copy.wait()
+    outputs = {(k, n): n + TAPS - 1 - k for n in range(LOCAL) for k in range(TAPS)}
     coarse_sums(
-        xt_ref, proto_ref, w_ref, (h0, h1, h2), (l0, l1, l2), sums_ref,
-        0, LOCAL, MAIN_OUT, 256,
+        xt_ref, proto_ref, w_ref, (h0, h1, h2), (l0, l1, l2), sums_ref, outputs,
     )
     beam_and_deal(
-        lambda row, tile: sums_ref[row : row + 8, (3 + tile) * 128 : (3 + tile) * 128 + 128],
-        jones_ref, dealt_ref, 4, 3, 64,
+        lambda row, tile: sums_ref[row : row + 8, tile * 128 : tile * 128 + 128],
+        jones_ref, dealt_ref, TILES, 2 * ROWS,
     )
     for d in range(8):
         for h in range(2):
-            out_ref[d, h] = dealt_ref[d * 64 + h * 32 : d * 64 + h * 32 + 32, :].astype(BF16)
-
-
-def edge_kernel(halo_ref, edge_ref, jones_ref, rest_ref, out_ref, dealt_ref):
-    def load(row, tile):
-        span = slice(tile * 128, tile * 128 + 128)
-        return halo_ref[row : row + 8, span] + edge_ref[row : row + 8, span]
-
-    beam_and_deal(load, jones_ref, dealt_ref, 3, 0, 48)
-    for d in range(8):
-        for h in range(2):
-            out_ref[d, h, 0:24, :] = dealt_ref[d * 48 + h * 24 : d * 48 + h * 24 + 24, :].astype(BF16)
-            out_ref[d, h, 24:56, :] = rest_ref[d, h]
+            first = (d * 2 + h) * ROWS
+            out_ref[d, h] = dealt_ref[first : first + ROWS, :].astype(BF16)
 
 
 def fine_table():
-    blocks, frames = 8, LOCAL
-    length = blocks * frames
-    k = np.arange(length)
-    angle = 2.0 * np.pi * ((k[:, None] * k[None, :]) % length) / length
-    cosine = np.cos(angle) / np.sqrt(length)
-    sine = np.sin(angle) / np.sqrt(length)
+    blocks = 8
+    length = blocks * LOCAL
     groups = length // GROUP
     table = np.zeros((blocks, ROWS, groups, 128))
-    view = table[:, : 2 * frames].reshape(blocks, frames, 2, groups, 128)
-    cosine = cosine.reshape(blocks, frames, groups, GROUP)
-    sine = sine.reshape(blocks, frames, groups, GROUP)
-    view[:, :, 0, :, :GROUP] = cosine
-    view[:, :, 1, :, :GROUP] = sine
-    view[:, :, 0, :, GROUP : 2 * GROUP] = -sine
-    view[:, :, 1, :, GROUP : 2 * GROUP] = cosine
-    table[:, : 2 * frames] = view.reshape(blocks, 2 * frames, groups, 128)
+    k = np.arange(length)
+    for block in range(blocks):
+        for local in range(SPREAD):
+            frame = block * LOCAL + local
+            if frame >= length:
+                continue
+            angle = 2.0 * np.pi * ((frame * k) % length) / length
+            cosine = (np.cos(angle) / np.sqrt(length)).reshape(groups, GROUP)
+            sine = (np.sin(angle) / np.sqrt(length)).reshape(groups, GROUP)
+            table[block, 2 * local, :, :GROUP] = cosine
+            table[block, 2 * local, :, GROUP : 2 * GROUP] = -sine
+            table[block, 2 * local + 1, :, :GROUP] = sine
+            table[block, 2 * local + 1, :, GROUP : 2 * GROUP] = cosine
     table = table.reshape(blocks * ROWS, groups * 128).astype(np.float32)
     high = table.astype(jnp.bfloat16)
     low = (table - high.astype(np.float32)).astype(jnp.bfloat16)
@@ -346,62 +327,30 @@
     return [pltpu.VMEM((rows, 256), BF16)] * 6
 
 
-def halo_call(x, proto, kept, beam):
+def front_call(x, proto, kept, beam):
+    rows = TILES * 128
     return pl.pallas_call(
-        halo_kernel,
-        out_shape=(
-            jax.ShapeDtypeStruct((256, FRAME), BF16),
-            jax.ShapeDtypeStruct((128, EDGE * SIGS), F32),
-            jax.ShapeDtypeStruct((LOCAL * COLS, SIGS, 128), BF16),
-            jax.ShapeDtypeStruct(proto.shape, F32),
-            jax.ShapeDtypeStruct(beam.shape, F32),
-        ),
+        front_kernel,
+        out_shape=jax.ShapeDtypeStruct((8, 2, ROWS, 128), BF16),
         in_specs=[anywhere()] * 4,
-        out_specs=(vmem(),) * 5,
+        out_specs=vmem(),
         scratch_shapes=[
+            pltpu.VMEM((LOCAL * COLS, SIGS, 128), BF16),
+            pltpu.VMEM(proto.shape, F32),
+            pltpu.VMEM(beam.shape, F32),
             pltpu.VMEM((1, KEPT), jnp.int32),
-            pltpu.VMEM((KEPT, 128), F32),
-            pltpu.VMEM((128, 512), F32),
-            *columns(512),
-            pltpu.SemaphoreType.DMA((2, 16)),
+            pltpu.VMEM((256, FRAME), BF16),
+            pltpu.VMEM((4 * KEPT, 128), F32),
+            pltpu.VMEM((2 * KEPT, 128), F32),
+            pltpu.VMEM((128, rows), F32),
+            pltpu.VMEM((16 * ROWS, 128), F32),
+            *[pltpu.VMEM((rows, 256), BF16)] * 6,
+            pltpu.SemaphoreType.DMA((16,)),
             pltpu.SemaphoreType.DMA((3,)),
         ],
-        compiler_params=granted(8),
-        name="halo",
+        compiler_params=granted(16),
+        name="front",
     )(x, proto, kept, beam)
-
-
-def main_call(xt, proto, table, beam):
-    return pl.pallas_call(
-        main_kernel,
-        out_shape=(
-            jax.ShapeDtypeStruct((128, 1024), F32),
-            jax.ShapeDtypeStruct((4 * KEPT, 128), F32),
-            jax.ShapeDtypeStruct((8, 2, 32, 128), BF16),
-        ),
-        in_specs=[vmem()] * 4,
-        out_specs=(vmem(),) * 3,
-        scratch_shapes=[
-            *columns(1024),
-            pltpu.VMEM((8 * 64, 128), F32),
-            pltpu.VMEM((2 * KEPT, 128), F32),
-        ],
-        compiler_params=granted(14),
-        cost_estimate=pl.CostEstimate(flops=10**9, bytes_accessed=4 * 10**6, transcendentals=0),
-        name="main",
-    )(xt, proto, table, beam)
-
-
-def edge_call(halo, edge, jones, rest):
-    return pl.pallas_call(
-        edge_kernel,
-        out_shape=jax.ShapeDtypeStruct((8, 2, ROWS, 128), BF16),
-        in_specs=[vmem()] * 4,
-        out_specs=vmem(),
-        scratch_shapes=[pltpu.VMEM((8 * 48, 128), F32)],
-        compiler_params=granted(4),
-        name="edge",
-    )(halo, edge, jones, rest)
 
 
 def fine_call(turned, table):
@@ -441,16 +390,12 @@
 def shards(voltages, prototype, kept_channels, beam_jones, station_map, tile_pairs):
     stations = voltages.shape[0]
     x = voltages.reshape(stations, 2, LOCAL * COLS, 128).transpose(0, 2, 1, 3)
-    table, halo, xt, proto, beam = halo_call(
+    beamed = front_call(
         kept_in_hbm(x),
         kept_in_hbm(prototype),
         kept_in_hbm(kept_channels.reshape(1, KEPT)),
         kept_in_hbm(beam_jones.reshape(128, KEPT)),
     )
-    blocks = lax.axis_size("tm")
-    halo = lax.ppermute(halo, "tm", [(n, n + 1) for n in range(blocks - 1)])
-    sums, jones, rest = main_call(xt, proto, table, beam)
-    beamed = edge_call(halo, sums, jones, rest)
     turned = lax.all_to_all(beamed, "tm", 0, 0, tiled=True)
     fine = fine_call(turned, jnp.asarray(fine_table()))
     fine = fine.reshape(32, 16, 2, 128)

time: 50.8 us -> 47.5 us (0.935)
  starting transfers between devices: 1.75 us -> 0 us
  Pallas kernels: 13.4 us -> 11.8 us
    ppermute x1 -> x0, starting transfers between devices: 1.75 us -> none  [shards(): halo = lax.ppermute(halo, 'tm', [(n, n + 1) for n in range(blocks - 1)])]
    pallas_call x3 -> x1, Pallas kernels: 8.63 us -> 6.93 us  [front_call(): pl.pallas_call(front_kernel, out_shape=jax.ShapeDtypeStruct((8, 2, ROWS,...]
  transfers between devices with their start and end apart: 1 -> 0, of which waited for: 0 -> 0; matrix products, arithmetic and copies ran while one was open for 0% -> 0% of each run, Pallas kernels for 8% -> 0%
where the time goes in v2:
time: 47.5 us; the launch traced here: 47.4 us
  blocking collectives  35.5 us (75%)
  Pallas kernels  11.8 us (25%)
    all_to_all x1, blocking collectives, shards(): rows = lax.all_to_all(fine, 'stn', 0, 0, tiled=True)  23.2 us
    all_to_all x1, blocking collectives, shards(): turned = lax.all_to_all(beamed, 'tm', 0, 0, tiled=True)  12.3 us
    pallas_call x1, Pallas kernels, front_call(): pl.pallas_call(front_kernel, out_shape=jax.ShapeDtypeStruct((8, 2, ROWS,...  6.93 us
    pallas_call x1, Pallas kernels, pairs_call(): pl.pallas_call(pairs_kernel, out_shape=jax.ShapeDtypeStruct((1, tiles, 2,...  4.24 us

profile of v2, /device:TPU:32, one launch (start us, length us, event | category | flops | bytes accessed | tf_op | source)
XLA Modules:
  0.0 47.4 jit_solution(11435236175122183902)
XLA Ops:
  0.0 0.0 copy-start
  0.0 6.9 %front.1 = bf16[8,2,80,128]{3,2,1,0:T(8,128)(2,1)S(1)} custom-call(bf16[16,162,2,128]{3,2,1,0:T(2,128)(2,1)} %bitcast.11, f32[12,768]{1,0:T(8,128)} %proto_in.1, s32[1,64]{1,0:T(1,128)} %bitcast.13, f32[128,64]{1,0:T(8,128)} %bitcast.12), custom_call_target="tpu_custom_call" | custom-call | tf_op jit(solution)/shard_map/front/pallas_call | solution.py:332
  6.9 12.3 %all_to_all.10.x_ref = bf16[8,2,80,128]{3,2,1,0:T(8,128)(2,1)S(1)} all-to-all(bf16[8,2,80,128]{3,2,1,0:T(8,128)(2,1)S(1)} %front.1), channel_id=1, replica_groups=mesh['tm'=8,'stn'=32] {'tm'}, dimensions={0} | all-to-all | bytes 655360 | tf_op jit(solution)/shard_map/all_to_all | solution.py:399
  19.2 0.0 copy-done
  19.2 0.0 copy-start.1
  19.3 0.0 copy-start.2
  19.3 0.6 %fine.1 = bf16[32,32,128]{2,1,0:T(8,128)(2,1)S(1)} custom-call(bf16[8,2,80,128]{3,2,1,0:T(8,128)(2,1)S(1)} %all_to_all.10.x_ref, bf16[2,640,512]{2,1,0:T(8,128)(2,1)S(1)} %copy-done), custom_call_target="tpu_custom_call" | custom-call | tf_op jit(solution)/shard_map/fine/pallas_call | solution.py:357
  19.9 23.2 %all_to_all.11 = bf16[32,16,2,128]{3,2,1,0:T(2,128)(2,1)S(1)} all-to-all(bf16[32,16,2,128]{3,2,1,0:T(2,128)(2,1)S(1)} %bitcast.9), channel_id=1, replica_groups=mesh['tm'=8,'stn'=32] {'stn'}, dimensions={0} | all-to-all | bytes 524288 | tf_op jit(solution)/shard_map/all_to_all | solution.py:402
  43.1 0.0 copy-done.1
  43.1 0.0 copy-done.2
  43.1 4.2 %pairs.1 = f32[1,36,2,128,128]{4,3,2,1,0:T(8,128)} custom-call(s32[512]{0:T(512)S(1)} %copy-done.1, s32[2,36]{1,0:T(2,128)S(1)} %bitcast.10, bf16[512,2,128]{2,1,0:T(2,128)(2,1)S(1)} %bitcast.8), custom_call_target="tpu_custom_call" | custom-call | tf_op jit(solution)/shard_map/pairs/pallas_call | solution.py:369
Async XLA Ops:
  0.0 19.2 %copy-start = (bf16[2,640,512]{2,1,0:T(8,128)(2,1)S(1)}, bf16[2,640,512]{2,1,0:T(8,128)(2,1)}, u32[]{:S(2)}) copy-start(bf16[2,640,512]{2,1,0:T(8,128)(2,1)} %constant.2.clone.table_ref) | copy-start | bytes 3932164
  19.2 23.9 %copy-start.1 = (s32[512]{0:T(512)S(1)}, s32[512]{0:T(512)}, u32[]{:S(2)}) copy-start(s32[512]{0:T(512)} %map_ref.1) | copy-start | bytes 6148
  19.3 23.9 %copy-start.2 = (s32[36,2]{0,1:T(2,128)S(1)}, s32[36,2]{0,1:T(2,128)}, u32[]{:S(2)}) copy-start(s32[36,2]{0,1:T(2,128)} %param.12) | copy-start | bytes 868

commit v3 on v2

--- a/solution.py
+++ b/solution.py
@@ -17,7 +17,8 @@
 LOCAL = 27
 SPREAD = LOCAL + TAPS - 1
 TILES = 10
-STEPS = 5
+STEPS = 10
+PADDED = 1536
 SIGS = 32
 KEPT = 64
 ROWS = 80
@@ -112,9 +113,7 @@
 
 
 def coarse_sums(x_ref, proto_ref, w_ref, highs, lows, sums_ref, outputs):
-    chunk = TILES * 128 // STEPS
-
-    def transform(pair, q):
+    def transform(pair, q, chunk):
         rows = pl.ds(pl.multiple_of(q * chunk, chunk), chunk)
         span = slice(pair * 256, pair * 256 + 256)
         both = lax.dot_general(
@@ -130,20 +129,17 @@
 
     for pair in range(COLS // 2):
 
-        if pair > 0:
-            transform(pair - 1, STEPS - 1)
-
         @pl.loop(0, 4)
         def _(q):
             if pair > 0:
-                transform(pair - 1, q)
+                transform(pair - 1, q, PADDED // 4)
             filter_column(
                 x_ref, proto_ref, highs[pair], lows[pair],
                 pair * 2 + q // 2, q % 2, q // 2, outputs,
             )
 
     for q in range(STEPS):
-        transform(COLS // 2 - 1, q)
+        transform(COLS // 2 - 1, q, TILES * 128 // STEPS)
 
 
 def beam_and_deal(load, jones_ref, dealt_ref, tiles, stride):
@@ -273,36 +269,41 @@
     return np.stack([high, low])
 
 
-def fine_kernel(x_ref, table_ref, out_ref):
+def fine_kernel(x_ref, table_ref, out_ref, fine_ref):
     for h in range(2):
         rows = x_ref[:, h].astype(F32).reshape(8 * ROWS, 128)
         turned = rows.T.astype(BF16)
         fine = lax.dot_general(turned, table_ref[0], NN, preferred_element_type=F32)
         fine = fine + lax.dot_general(turned, table_ref[1], NN, preferred_element_type=F32)
+        for g in range(4):
+            fine_ref[h, g] = fine[:, g * 128 : g * 128 + 128]
         for j in range(4):
             for g in range(4):
-                piece = fine[j * 32 : j * 32 + 32, g * 128 : g * 128 + 128]
-                out_ref[(h * 4 + j) * 4 + g] = piece.astype(BF16)
+                for pol in range(2):
+                    piece = fine_ref[h, g, pl.ds(j * SIGS + pol, 16, stride=2), :]
+                    out_ref[(h * 4 + j) * 4 + g, :, pol * 128 : pol * 128 + 128] = piece.astype(BF16)
 
 
 def pairs_kernel(map_ref, pairs_ref, x_ref, out_ref, ordered_ref, own_ref, turned_ref, made, sems):
     tiles = made.shape[0]
-    rows = ordered_ref.reshape(1024, 128)
-
-    @pl.loop(0, 512, unroll=8)
-    def _(row):
-        ordered_ref[map_ref[row]] = x_ref[row]
-
-    lane = lax.broadcasted_iota(jnp.int32, (128, 128), 1)
-    for block in range(8):
-        span = slice(block * 128, block * 128 + 128)
-        own = rows[span, :]
-        own_ref[span, :] = own
-        value = own.astype(F32)
-        turned = jnp.where(
-            lane < GROUP, -pltpu.roll(value, 128 - GROUP, 1), pltpu.roll(value, GROUP, 1)
-        )
-        turned_ref[span, :] = turned.astype(BF16)
+    stations = x_ref.shape[0]
+    place = lax.broadcasted_iota(jnp.int32, (BLOCK, stations), 0)
+    lane = lax.broadcasted_iota(jnp.int32, (BLOCK, 128), 1)
+    for part in range(stations // BLOCK):
+        chosen = jnp.where(map_ref[...] == place + part * BLOCK, 1.0, 0.0).astype(BF16)
+        rows = lax.dot_general(chosen, x_ref[...], NN, preferred_element_type=F32)
+        for pol in range(2):
+            ordered_ref[pl.ds(part * 2 * BLOCK + pol, BLOCK, stride=2), :] = rows[
+                :, pol * 128 : pol * 128 + 128
+            ]
+        for block in range(2):
+            span = slice((part * 2 + block) * BLOCK, (part * 2 + block + 1) * BLOCK)
+            value = ordered_ref[span, :]
+            own_ref[span, :] = value.astype(BF16)
+            turned = jnp.where(
+                lane < GROUP, -pltpu.roll(value, 128 - GROUP, 1), pltpu.roll(value, GROUP, 1)
+            )
+            turned_ref[span, :] = turned.astype(BF16)
 
     def send(tile):
         return pltpu.make_async_copy(made.at[tile], out_ref.at[0, tile], sems.at[tile])
@@ -328,7 +329,6 @@
 
 
 def front_call(x, proto, kept, beam):
-    rows = TILES * 128
     return pl.pallas_call(
         front_kernel,
         out_shape=jax.ShapeDtypeStruct((8, 2, ROWS, 128), BF16),
@@ -342,9 +342,9 @@
             pltpu.VMEM((256, FRAME), BF16),
             pltpu.VMEM((4 * KEPT, 128), F32),
             pltpu.VMEM((2 * KEPT, 128), F32),
-            pltpu.VMEM((128, rows), F32),
+            pltpu.VMEM((128, PADDED), F32),
             pltpu.VMEM((16 * ROWS, 128), F32),
-            *[pltpu.VMEM((rows, 256), BF16)] * 6,
+            *[pltpu.VMEM((PADDED, 256), BF16)] * 6,
             pltpu.SemaphoreType.DMA((16,)),
             pltpu.SemaphoreType.DMA((3,)),
         ],
@@ -356,9 +356,10 @@
 def fine_call(turned, table):
     return pl.pallas_call(
         fine_kernel,
-        out_shape=jax.ShapeDtypeStruct((32, SIGS, 128), BF16),
+        out_shape=jax.ShapeDtypeStruct((32, 16, 256), BF16),
         in_specs=[vmem()] * 2,
         out_specs=vmem(),
+        scratch_shapes=[pltpu.VMEM((2, 4, 128, 128), F32)],
         compiler_params=granted(8),
         name="fine",
     )(turned, table)
@@ -369,10 +370,10 @@
     return pl.pallas_call(
         pairs_kernel,
         out_shape=jax.ShapeDtypeStruct((1, tiles, 2, BLOCK, BLOCK), F32),
-        in_specs=[smem(), smem(), vmem()],
+        in_specs=[vmem(), smem(), vmem()],
         out_specs=anywhere(),
         scratch_shapes=[
-            pltpu.VMEM((512, 2, 128), BF16),
+            pltpu.VMEM((1024, 128), F32),
             pltpu.VMEM((1024, 128), BF16),
             pltpu.VMEM((1024, 128), BF16),
             pltpu.VMEM((tiles, 2, BLOCK, BLOCK), F32),
@@ -398,9 +399,8 @@
     )
     turned = lax.all_to_all(beamed, "tm", 0, 0, tiled=True)
     fine = fine_call(turned, jnp.asarray(fine_table()))
-    fine = fine.reshape(32, 16, 2, 128)
     rows = lax.all_to_all(fine, "stn", 0, 0, tiled=True)
-    return pairs_call(station_map, tile_pairs.T, rows.reshape(512, 2, 128))
+    return pairs_call(station_map.reshape(1, -1), tile_pairs.T, rows.reshape(-1, 256))
 
 
 def solution(mesh):

time: 47.5 us -> 46.7 us (0.983)
  Pallas kernels: 11.8 us -> 10.9 us
    pallas_call x1, Pallas kernels: 4.24 us -> 3.71 us  [pairs_call(): pl.pallas_call(pairs_kernel, out_shape=jax.ShapeDtypeStruct((1, tiles, 2,...]
where the time goes in v3:
time: 46.7 us; the launch traced here: 46.5 us
  blocking collectives  35.5 us (76%)
  Pallas kernels  10.9 us (23%)
    all_to_all x1, blocking collectives, shards(): rows = lax.all_to_all(fine, 'stn', 0, 0, tiled=True)  23.3 us
    all_to_all x1, blocking collectives, shards(): turned = lax.all_to_all(beamed, 'tm', 0, 0, tiled=True)  12.3 us
    pallas_call x1, Pallas kernels, front_call(): pl.pallas_call(front_kernel, out_shape=jax.ShapeDtypeStruct((8, 2, ROWS,...  6.55 us
    pallas_call x1, Pallas kernels, pairs_call(): pl.pallas_call(pairs_kernel, out_shape=jax.ShapeDtypeStruct((1, tiles, 2,...  3.71 us

profile of v3, /device:TPU:32, one launch (start us, length us, event | category | flops | bytes accessed | tf_op | source)
XLA Modules:
  0.0 46.5 jit_solution(3910959311747923668)
XLA Ops:
  0.0 0.0 copy-start
  0.0 6.5 %front.1 = bf16[8,2,80,128]{3,2,1,0:T(8,128)(2,1)S(1)} custom-call(bf16[16,162,2,128]{3,2,1,0:T(2,128)(2,1)} %bitcast.11, f32[12,768]{1,0:T(8,128)} %proto_in.1, s32[1,64]{1,0:T(1,128)} %bitcast.13, f32[128,64]{1,0:T(8,128)} %bitcast.12), custom_call_target="tpu_custom_call" | custom-call | tf_op jit(solution)/shard_map/front/pallas_call | solution.py:332
  6.6 12.3 %all_to_all.10.x_ref = bf16[8,2,80,128]{3,2,1,0:T(8,128)(2,1)S(1)} all-to-all(bf16[8,2,80,128]{3,2,1,0:T(8,128)(2,1)S(1)} %front.1), channel_id=1, replica_groups=mesh['tm'=8,'stn'=32] {'tm'}, dimensions={0} | all-to-all | bytes 655360 | tf_op jit(solution)/shard_map/all_to_all | solution.py:400
  18.9 0.0 copy-done
  18.9 0.0 copy-start.1
  18.9 0.0 copy-start.2
  18.9 0.7 %fine.1 = bf16[32,16,256]{2,1,0:T(8,128)(2,1)S(1)} custom-call(bf16[8,2,80,128]{3,2,1,0:T(8,128)(2,1)S(1)} %all_to_all.10.x_ref, bf16[2,640,512]{2,1,0:T(8,128)(2,1)S(1)} %copy-done), custom_call_target="tpu_custom_call" | custom-call | tf_op jit(solution)/shard_map/fine/pallas_call | solution.py:357
  19.5 23.3 %all_to_all.11 = bf16[32,16,256]{2,1,0:T(8,128)(2,1)S(1)} all-to-all(bf16[32,16,256]{2,1,0:T(8,128)(2,1)S(1)} %fine.1), channel_id=1, replica_groups=mesh['tm'=8,'stn'=32] {'stn'}, dimensions={0} | all-to-all | bytes 524288 | tf_op jit(solution)/shard_map/all_to_all | solution.py:402
  42.8 0.0 copy-done.1
  42.8 0.0 copy-done.2
  42.8 3.7 %pairs.1 = f32[1,36,2,128,128]{4,3,2,1,0:T(8,128)} custom-call(s32[1,512]{1,0:T(1,128)S(1)} %bitcast.9, s32[2,36]{1,0:T(2,128)S(1)} %bitcast.10, bf16[512,256]{1,0:T(8,128)(2,1)S(1)} %bitcast.8), custom_call_target="tpu_custom_call" | custom-call | tf_op jit(solution)/shard_map/pairs/pallas_call | solution.py:370
Async XLA Ops:
  0.0 18.9 %copy-start = (bf16[2,640,512]{2,1,0:T(8,128)(2,1)S(1)}, bf16[2,640,512]{2,1,0:T(8,128)(2,1)}, u32[]{:S(2)}) copy-start(bf16[2,640,512]{2,1,0:T(8,128)(2,1)} %constant.2.clone.table_ref) | copy-start | bytes 3932164
  18.9 23.9 %copy-start.1 = (s32[512]{0:T(512)S(1)}, s32[512]{0:T(512)}, u32[]{:S(2)}) copy-start(s32[512]{0:T(512)} %param.11) | copy-start | bytes 6148
  18.9 23.9 %copy-start.2 = (s32[36,2]{0,1:T(2,128)S(1)}, s32[36,2]{0,1:T(2,128)}, u32[]{:S(2)}) copy-start(s32[36,2]{0,1:T(2,128)} %param.12) | copy-start | bytes 868

commit v4 on v3

--- a/solution.py
+++ b/solution.py
@@ -18,6 +18,8 @@
 SPREAD = LOCAL + TAPS - 1
 TILES = 10
 STEPS = 10
+FIRST_TM = 5
+FIRST_STN = 22
 PADDED = 1536
 SIGS = 32
 KEPT = 64
@@ -242,7 +244,7 @@
     for d in range(8):
         for h in range(2):
             first = (d * 2 + h) * ROWS
-            out_ref[d, h] = dealt_ref[first : first + ROWS, :].astype(BF16)
+            out_ref[(d - FIRST_TM) % 8, h] = dealt_ref[first : first + ROWS, :].astype(BF16)
 
 
 def fine_table():
@@ -263,6 +265,7 @@
             table[block, 2 * local, :, GROUP : 2 * GROUP] = -sine
             table[block, 2 * local + 1, :, :GROUP] = sine
             table[block, 2 * local + 1, :, GROUP : 2 * GROUP] = cosine
+    table = np.roll(table, -FIRST_TM, axis=0)
     table = table.reshape(blocks * ROWS, groups * 128).astype(np.float32)
     high = table.astype(jnp.bfloat16)
     low = (table - high.astype(np.float32)).astype(jnp.bfloat16)
@@ -281,16 +284,18 @@
             for g in range(4):
                 for pol in range(2):
                     piece = fine_ref[h, g, pl.ds(j * SIGS + pol, 16, stride=2), :]
-                    out_ref[(h * 4 + j) * 4 + g, :, pol * 128 : pol * 128 + 128] = piece.astype(BF16)
+                    at = ((h * 4 + j) * 4 + g - FIRST_STN) % 32
+                    out_ref[at, :, pol * 128 : pol * 128 + 128] = piece.astype(BF16)
 
 
 def pairs_kernel(map_ref, pairs_ref, x_ref, out_ref, ordered_ref, own_ref, turned_ref, made, sems):
     tiles = made.shape[0]
     stations = x_ref.shape[0]
+    placed = pltpu.roll(map_ref[...], stations - FIRST_STN * (stations // 32), 1)
     place = lax.broadcasted_iota(jnp.int32, (BLOCK, stations), 0)
     lane = lax.broadcasted_iota(jnp.int32, (BLOCK, 128), 1)
     for part in range(stations // BLOCK):
-        chosen = jnp.where(map_ref[...] == place + part * BLOCK, 1.0, 0.0).astype(BF16)
+        chosen = jnp.where(placed == place + part * BLOCK, 1.0, 0.0).astype(BF16)
         rows = lax.dot_general(chosen, x_ref[...], NN, preferred_element_type=F32)
         for pol in range(2):
             ordered_ref[pl.ds(part * 2 * BLOCK + pol, BLOCK, stride=2), :] = rows[
@@ -388,6 +393,12 @@
     return pltpu.with_memory_space_constraint(value, pltpu.HBM)
 
 
+def exchange(value, axis, first):
+    count = lax.axis_size(axis)
+    group = [(first + n) % count for n in range(count)]
+    return lax.all_to_all(value, axis, 0, 0, tiled=True, axis_index_groups=[group])
+
+
 def shards(voltages, prototype, kept_channels, beam_jones, station_map, tile_pairs):
     stations = voltages.shape[0]
     x = voltages.reshape(stations, 2, LOCAL * COLS, 128).transpose(0, 2, 1, 3)
@@ -397,9 +408,9 @@
         kept_in_hbm(kept_channels.reshape(1, KEPT)),
         kept_in_hbm(beam_jones.reshape(128, KEPT)),
     )
-    turned = lax.all_to_all(beamed, "tm", 0, 0, tiled=True)
+    turned = exchange(beamed, "tm", FIRST_TM)
     fine = fine_call(turned, jnp.asarray(fine_table()))
-    rows = lax.all_to_all(fine, "stn", 0, 0, tiled=True)
+    rows = exchange(fine, "stn", FIRST_STN)
     return pairs_call(station_map.reshape(1, -1), tile_pairs.T, rows.reshape(-1, 256))
 
 

time: 46.7 us -> 41.1 us (0.88)
  the two profiles are of different devices: /device:TPU:32 before, /device:TPU:4 now
where the time goes in v4:
time: 41.1 us; the launch traced here: 41 us
  blocking collectives  30 us (73%)
  Pallas kernels  11 us (27%)
    all_to_all x2, blocking collectives, exchange(): lax.all_to_all(value, axis, 0, 0, tiled=True, axis_index_groups=[group])  30 us
    pallas_call x1, Pallas kernels, front_call(): pl.pallas_call(front_kernel, out_shape=jax.ShapeDtypeStruct((8, 2, ROWS,...  6.54 us
    pallas_call x1, Pallas kernels, pairs_call(): pl.pallas_call(pairs_kernel, out_shape=jax.ShapeDtypeStruct((1, tiles, 2,...  3.76 us

profile of v4, /device:TPU:4, one launch (start us, length us, event | category | flops | bytes accessed | tf_op | source)
XLA Modules:
  0.0 41.0 jit_solution(6131501407517328996)
XLA Ops:
  0.0 0.0 copy-start
  0.0 6.5 %front.1 = bf16[8,2,80,128]{3,2,1,0:T(8,128)(2,1)S(1)} custom-call(bf16[16,162,2,128]{3,2,1,0:T(2,128)(2,1)} %bitcast.11, f32[12,768]{1,0:T(8,128)} %proto_in.1, s32[1,64]{1,0:T(1,128)} %bitcast.13, f32[128,64]{1,0:T(8,128)} %bitcast.12), custom_call_target="tpu_custom_call" | custom-call | tf_op jit(solution)/shard_map/front/pallas_call | solution.py:337
  6.6 11.2 %all_to_all.10.x_ref = bf16[8,2,80,128]{3,2,1,0:T(8,128)(2,1)S(1)} all-to-all(bf16[8,2,80,128]{3,2,1,0:T(8,128)(2,1)S(1)} %front.1), channel_id=1, replica_groups={{160,192,224,0,32,64,96,128},{161,193,225,1,33,65,97,129},{162,194,226,..., dimensions={0} | all-to-all | bytes 655360 | tf_op jit(solution)/shard_map/all_to_all | solution.py:399
  17.8 0.0 copy-done
  17.8 0.0 copy-start.1
  17.8 0.0 copy-start.2
  17.8 0.7 %fine.1 = bf16[32,16,256]{2,1,0:T(8,128)(2,1)S(1)} custom-call(bf16[8,2,80,128]{3,2,1,0:T(8,128)(2,1)S(1)} %all_to_all.10.x_ref, bf16[2,640,512]{2,1,0:T(8,128)(2,1)S(1)} %copy-done), custom_call_target="tpu_custom_call" | custom-call | tf_op jit(solution)/shard_map/fine/pallas_call | solution.py:362
  18.4 18.8 %all_to_all.11 = bf16[32,16,256]{2,1,0:T(8,128)(2,1)S(1)} all-to-all(bf16[32,16,256]{2,1,0:T(8,128)(2,1)S(1)} %fine.1), channel_id=1, replica_groups={{22,23,24,25,26,27,28,29,30,31,0,1,2,3,4,5,6,7,8,9,10,11,12,13,14,15,16..., dimensions={0} | all-to-all | bytes 524288 | tf_op jit(solution)/shard_map/all_to_all | solution.py:399
  37.2 0.0 copy-done.1
  37.2 0.0 copy-done.2
  37.2 3.8 %pairs.1 = f32[1,36,2,128,128]{4,3,2,1,0:T(8,128)} custom-call(s32[1,512]{1,0:T(1,128)S(1)} %bitcast.9, s32[2,36]{1,0:T(2,128)S(1)} %bitcast.10, bf16[512,256]{1,0:T(8,128)(2,1)S(1)} %bitcast.8), custom_call_target="tpu_custom_call" | custom-call | tf_op jit(solution)/shard_map/pairs/pallas_call | solution.py:375
Async XLA Ops:
  0.0 17.8 %copy-start = (bf16[2,640,512]{2,1,0:T(8,128)(2,1)S(1)}, bf16[2,640,512]{2,1,0:T(8,128)(2,1)}, u32[]{:S(2)}) copy-start(bf16[2,640,512]{2,1,0:T(8,128)(2,1)} %constant.2.clone.table_ref) | copy-start | bytes 3932164
  17.8 19.4 %copy-start.1 = (s32[512]{0:T(512)S(1)}, s32[512]{0:T(512)}, u32[]{:S(2)}) copy-start(s32[512]{0:T(512)} %param.11) | copy-start | bytes 6148
  17.8 19.4 %copy-start.2 = (s32[36,2]{0,1:T(2,128)S(1)}, s32[36,2]{0,1:T(2,128)}, u32[]{:S(2)}) copy-start(s32[36,2]{0,1:T(2,128)} %param.12) | copy-start | bytes 868

commit v5 on v4

--- a/solution.py
+++ b/solution.py
@@ -223,7 +223,9 @@
     ]
     kept_copy = pltpu.make_async_copy(kept_in, kept_ref, more.at[0])
     proto_copy = pltpu.make_async_copy(proto_in, proto_ref, more.at[1])
-    beam_copy = pltpu.make_async_copy(beam_in, beam_ref, more.at[2])
+    beam_copy = pltpu.make_async_copy(
+        beam_in, beam_ref.at[pl.ds(0, beam_in.shape[0])], more.at[2]
+    )
     for copy in [kept_copy, beam_copy, proto_copy] + rows:
         copy.start()
     clear((h0, h1, h2, l0, l1, l2), SPREAD * SIGS, TILES * 128)
@@ -279,7 +281,7 @@
         fine = lax.dot_general(turned, table_ref[0], NN, preferred_element_type=F32)
         fine = fine + lax.dot_general(turned, table_ref[1], NN, preferred_element_type=F32)
         for g in range(4):
-            fine_ref[h, g] = fine[:, g * 128 : g * 128 + 128]
+            fine_ref[h, g, :128, :] = fine[:, g * 128 : g * 128 + 128]
         for j in range(4):
             for g in range(4):
                 for pol in range(2):
@@ -342,13 +344,13 @@
         scratch_shapes=[
             pltpu.VMEM((LOCAL * COLS, SIGS, 128), BF16),
             pltpu.VMEM(proto.shape, F32),
-            pltpu.VMEM(beam.shape, F32),
+            pltpu.VMEM((beam.shape[0] + 8, beam.shape[1]), F32),
             pltpu.VMEM((1, KEPT), jnp.int32),
             pltpu.VMEM((256, FRAME), BF16),
             pltpu.VMEM((4 * KEPT, 128), F32),
-            pltpu.VMEM((2 * KEPT, 128), F32),
+            pltpu.VMEM((2 * KEPT + 16, 128), F32),
             pltpu.VMEM((128, PADDED), F32),
-            pltpu.VMEM((16 * ROWS, 128), F32),
+            pltpu.VMEM((18 * ROWS, 128), F32),
             *[pltpu.VMEM((PADDED, 256), BF16)] * 6,
             pltpu.SemaphoreType.DMA((16,)),
             pltpu.SemaphoreType.DMA((3,)),
@@ -364,7 +366,7 @@
         out_shape=jax.ShapeDtypeStruct((32, 16, 256), BF16),
         in_specs=[vmem()] * 2,
         out_specs=vmem(),
-        scratch_shapes=[pltpu.VMEM((2, 4, 128, 128), F32)],
+        scratch_shapes=[pltpu.VMEM((2, 4, 136, 128), F32)],
         compiler_params=granted(8),
         name="fine",
     )(turned, table)
@@ -378,7 +380,7 @@
         in_specs=[vmem(), smem(), vmem()],
         out_specs=anywhere(),
         scratch_shapes=[
-            pltpu.VMEM((1024, 128), F32),
+            pltpu.VMEM((1032, 128), F32),
             pltpu.VMEM((1024, 128), BF16),
             pltpu.VMEM((1024, 128), BF16),
             pltpu.VMEM((tiles, 2, BLOCK, BLOCK), F32),

time: 41.1 us -> 41.1 us (level)
  no operation moved by 1% of the time
where the time goes in v5:
time: 41.1 us; the launch traced here: 41 us
  blocking collectives  30 us (73%)
  Pallas kernels  10.9 us (27%)
    all_to_all x2, blocking collectives, exchange(): lax.all_to_all(value, axis, 0, 0, tiled=True, axis_index_groups=[group])  30 us
    pallas_call x1, Pallas kernels, front_call(): pl.pallas_call(front_kernel, out_shape=jax.ShapeDtypeStruct((8, 2, ROWS,...  6.52 us
    pallas_call x1, Pallas kernels, pairs_call(): pl.pallas_call(pairs_kernel, out_shape=jax.ShapeDtypeStruct((1, tiles, 2,...  3.76 us

profile of v5, /device:TPU:4, one launch (start us, length us, event | category | flops | bytes accessed | tf_op | source)
XLA Modules:
  0.0 41.0 jit_solution(7834358174338767218)
XLA Ops:
  0.0 0.0 copy-start
  0.0 6.5 %front.1 = bf16[8,2,80,128]{3,2,1,0:T(8,128)(2,1)S(1)} custom-call(bf16[16,162,2,128]{3,2,1,0:T(2,128)(2,1)} %bitcast.11, f32[12,768]{1,0:T(8,128)} %proto_in.1, s32[1,64]{1,0:T(1,128)} %bitcast.13, f32[128,64]{1,0:T(8,128)} %bitcast.12), custom_call_target="tpu_custom_call" | custom-call | tf_op jit(solution)/shard_map/front/pallas_call | solution.py:339
  6.5 11.2 %all_to_all.10.x_ref = bf16[8,2,80,128]{3,2,1,0:T(8,128)(2,1)S(1)} all-to-all(bf16[8,2,80,128]{3,2,1,0:T(8,128)(2,1)S(1)} %front.1), channel_id=1, replica_groups={{160,192,224,0,32,64,96,128},{161,193,225,1,33,65,97,129},{162,194,226,..., dimensions={0} | all-to-all | bytes 655360 | tf_op jit(solution)/shard_map/all_to_all | solution.py:401
  17.7 0.0 copy-done
  17.8 0.0 copy-start.1
  17.8 0.0 copy-start.2
  17.8 0.7 %fine.1 = bf16[32,16,256]{2,1,0:T(8,128)(2,1)S(1)} custom-call(bf16[8,2,80,128]{3,2,1,0:T(8,128)(2,1)S(1)} %all_to_all.10.x_ref, bf16[2,640,512]{2,1,0:T(8,128)(2,1)S(1)} %copy-done), custom_call_target="tpu_custom_call" | custom-call | tf_op jit(solution)/shard_map/fine/pallas_call | solution.py:364
  18.4 18.8 %all_to_all.11 = bf16[32,16,256]{2,1,0:T(8,128)(2,1)S(1)} all-to-all(bf16[32,16,256]{2,1,0:T(8,128)(2,1)S(1)} %fine.1), channel_id=1, replica_groups={{22,23,24,25,26,27,28,29,30,31,0,1,2,3,4,5,6,7,8,9,10,11,12,13,14,15,16..., dimensions={0} | all-to-all | bytes 524288 | tf_op jit(solution)/shard_map/all_to_all | solution.py:401
  37.2 0.0 copy-done.1
  37.2 0.0 copy-done.2
  37.2 3.8 %pairs.1 = f32[1,36,2,128,128]{4,3,2,1,0:T(8,128)} custom-call(s32[1,512]{1,0:T(1,128)S(1)} %bitcast.9, s32[2,36]{1,0:T(2,128)S(1)} %bitcast.10, bf16[512,256]{1,0:T(8,128)(2,1)S(1)} %bitcast.8), custom_call_target="tpu_custom_call" | custom-call | tf_op jit(solution)/shard_map/pairs/pallas_call | solution.py:377
Async XLA Ops:
  0.0 17.8 %copy-start = (bf16[2,640,512]{2,1,0:T(8,128)(2,1)S(1)}, bf16[2,640,512]{2,1,0:T(8,128)(2,1)}, u32[]{:S(2)}) copy-start(bf16[2,640,512]{2,1,0:T(8,128)(2,1)} %constant.2.clone.table_ref) | copy-start | bytes 3932164
  17.8 19.4 %copy-start.1 = (s32[512]{0:T(512)S(1)}, s32[512]{0:T(512)}, u32[]{:S(2)}) copy-start(s32[512]{0:T(512)} %param.11) | copy-start | bytes 6148
  17.8 19.4 %copy-start.2 = (s32[36,2]{0,1:T(2,128)S(1)}, s32[36,2]{0,1:T(2,128)}, u32[]{:S(2)}) copy-start(s32[36,2]{0,1:T(2,128)} %param.12) | copy-start | bytes 868
